TPU v7x, 32 devices: a whole 2x2x4 slice. The times are simulated.
32 devices in a mesh: leaf: 16 (over z, x, core), rhs: 2 (over y).
Axes of the slice: x: 2, y: 2, z: 4, core: 2. Of those that a mesh axis runs over, the one named last changes fastest.
Arguments:
- rhs: bfloat16 [131072, 512], P('leaf', 'rhs'), may hold values from -6 to 6
- source_basis: bfloat16 [1024, 128, 128], P('leaf', None, 'rhs'), may hold values from -0.5 to 0.5
- target_basis: bfloat16 [1024, 128, 128], P('leaf', None, 'rhs'), may hold values from -0.5 to 0.5
- near_blocks: bfloat16 [1024, 2, 128, 128], P('leaf', None, None, 'rhs'), may hold values from -0.375 to 0.375
- near_offsets: int32 [1024, 2], P('leaf'), may hold values from -2 to 2
- source_values: bfloat16 [3, 512, 2, 2, 128, 128], P(None, 'leaf', None, None, 'rhs'), may hold values from -0.375 to 0.375
- source_scales: float32 [3, 512, 2, 2, 128], P(None, 'leaf'), may hold values from 0.2 to 2
- target_values: bfloat16 [3, 512, 2, 2, 128, 128], P(None, 'leaf', None, None, 'rhs'), may hold values from -0.375 to 0.375
- target_scales: float32 [3, 512, 2, 2, 128], P(None, 'leaf'), may hold values from 0.2 to 2
Outputs:
- product: bfloat16 [131072, 512], P('leaf', 'rhs')
All inputs are finite; a program needn't handle non-finite values.
Results may differ from a plain program's by a relative error of at most 0.01.
Values may be sent and summed in bfloat16 or wider, within the bound.
No kernel may reach another device: no remote copies, remote signals or barrier semaphores. Data moves between devices by JAX's collectives and lax.ppermute only.
A program may use at most 192 MiB of HBM per device.

v0:
```python
import functools

import jax
import jax.numpy as jnp
from jax import lax
from jax.experimental import pallas as pl
from jax.experimental.pallas import tpu as pltpu
from jax.sharding import PartitionSpec as P

REACH = 2
SWAP = [(0, 1), (1, 0)]


def parity(value):
    return bin(value).count("1") & 1


def fill_level(weights, own, peer, scales, level, pairs, half, low, high):
    width = scales.shape[-1]
    for p in range(pairs):
        for o in range(2):
            for c in range(2):
                scale = scales[level, p, o, c : c + 1, :]
                for part, at in ((own, low), (peer, high)):
                    block = (part[level, p, o, c].astype(jnp.float32) * scale).astype(jnp.bfloat16)
                    start = pl.multiple_of(o * 2 * half + at, half)
                    weights[p, pl.ds(start, half), c * width : (c + 1) * width] = block


def mix_level(weights, read, write, level, pairs, rank):
    step = 2**level
    for p in range(pairs):
        i = (p >> level) * 2 * step + (p & (step - 1))
        j = i + step
        both = jnp.concatenate([read(i), read(j)], axis=0)
        mixed = jnp.dot(weights[p], both, preferred_element_type=jnp.float32).astype(jnp.bfloat16)
        write(i, mixed[:rank])
        write(j, mixed[rank:])


def source_kernel(idx, rhs_own, rhs_peer, basis_own, basis_peer, own, peer, scales, out, weights, state):
    boxes, rank, _ = out.shape
    rows = basis_own.shape[2]
    half = basis_own.shape[1]
    levels = own.shape[0]
    pairs = boxes // 2
    low = idx[1] * half
    high = (1 - idx[1]) * half
    for b in range(boxes):
        here = pl.ds(b * rows, rows)
        box = jnp.concatenate([rhs_own[here, :], rhs_peer[here, :]], axis=1)
        for part, at in ((basis_own, low), (basis_peer, high)):
            start = pl.multiple_of(b * rank + at, half)
            state[pl.ds(start, half), :] = jnp.dot(
                part[b], box, preferred_element_type=jnp.float32
            ).astype(jnp.bfloat16)

    def read(i):
        return state[i * rank : (i + 1) * rank, :]

    def write_state(i, value):
        state[i * rank : (i + 1) * rank, :] = value

    def write_out(i, value):
        out[i] = value

    for level in range(levels):
        fill_level(weights, own, peer, scales, level, pairs, half, low, high)
        mix_level(weights, read, write_out if level == levels - 1 else write_state, level, pairs, rank)


def target_kernel(
    idx, offsets, mixed, own, peer, scales, basis_own, basis_peer, near_own, near_peer, win_own, win_peer,
    *rest, first,
):
    prod, send, weights, state, left = rest if first else rest[1:]
    boxes, rank, _ = mixed.shape
    half = basis_own.shape[1]
    rows = basis_own.shape[2]
    near_count = near_own.shape[1]
    levels = own.shape[0]
    pairs = boxes // 2
    columns = prod.shape[1]
    low = idx[1] * half
    high = (1 - idx[1]) * half
    step = pl.program_id(0)

    def read_in(i):
        return mixed[i]

    def read_state(i):
        return state[i * rank : (i + 1) * rank, :]

    def write_state(i, value):
        state[i * rank : (i + 1) * rank, :] = value

    for level in range(levels):
        fill_level(weights, own, peer, scales, level, pairs, half, low, high)
        mix_level(weights, read_state if level else read_in, write_state, level, pairs, rank)
    first_box = idx[0] * boxes * pl.num_programs(0) + step * boxes
    for b in range(boxes):
        parts = [read_state(b)]
        for k in range(near_count):
            at = (step * boxes + b + REACH + offsets[(first_box + b) * near_count + k]) * rows
            there = pl.ds(pl.multiple_of(at, rows), rows)
            parts.append(jnp.concatenate([win_own[there, :], win_peer[there, :]], axis=1))
        for k in range(near_count + 1):
            for basis, near, at in ((basis_own, near_own, low), (basis_peer, near_peer, high)):
                start = pl.multiple_of(k * 2 * half + at, half)
                left[b, pl.ds(start, half), :] = near[b, k - 1] if k else basis[b]
        right = jnp.concatenate(parts, axis=0)
        total = lax.dot_general(
            left[b], right, (((0,), (0,)), ((), ())), preferred_element_type=jnp.float32
        ).astype(jnp.bfloat16)
        here = pl.ds(b * rows, rows)
        prod[here, :] = total[:, :columns]
        send[here, :] = total[:, columns:]


def edge_kernel(meta, near_own, near_peer, *rest):
    *boxes, out = rest
    half = near_own.shape[2]
    count = pl.num_programs(0)
    j = pl.program_id(0)
    h = meta[0]
    total = jnp.zeros(out.shape, jnp.float32)
    for k, box in enumerate(boxes):
        part = jnp.zeros(out.shape, jnp.float32)
        for near, at in ((near_own, h * half), (near_peer, (1 - h) * half)):
            part += lax.dot_general(
                near[0, k], box[pl.ds(pl.multiple_of(at, half), half), :], (((0,), (0,)), ((), ())),
                preferred_element_type=jnp.float32,
            )
        reads = meta[1 + count + (len(boxes) + k) * count + j]
        total += jnp.where(reads > 0, part, 0.0)
    out[...] = total


def on_device(
    rhs,
    source_basis,
    target_basis,
    near_blocks,
    near_offsets,
    source_values,
    source_scales,
    target_values,
    target_scales,
):
    leafs = lax.axis_size("leaf")
    box_count, rows, half = source_basis.shape
    columns = rhs.shape[1]
    levels = source_values.shape[0]
    rank = source_values.shape[5]
    near_count = near_blocks.shape[1]
    group = 2**levels
    chunk = 2 * group
    chunks = box_count // chunk
    quota = box_count // leafs
    span = chunk // quota
    bits = span.bit_length() - 1
    steps = chunks // 2
    masks = [[m for m in range(chunks - 1, -1, -1) if parity(m) == h] for h in range(2)]

    d = lax.axis_index("leaf")
    h = lax.axis_index("rhs")
    home = d >> bits
    mine = [home ^ jnp.where(h == 0, masks[0][s], masks[1][s]) for s in range(steps)]
    others = [home ^ jnp.where(h == 0, masks[1][s], masks[0][s]) for s in range(steps)]
    home_parity = sum(((home >> k) & 1) for k in range(chunks.bit_length())) & 1

    source_t = jnp.swapaxes(source_basis, 1, 2)
    target_t = jnp.swapaxes(target_basis, 1, 2)
    near_t = jnp.swapaxes(near_blocks, 2, 3)

    def cut(array, at, size, axis=0):
        return lax.dynamic_slice_in_dim(array, at * size, size, axis)

    def swap(array):
        return lax.ppermute(array, "rhs", SWAP)

    edges = [i for i in range(chunks - 1) if parity(i) != parity(i + 1)]
    assert edges == list(range(0, chunks, 2))
    owns = [(home_parity ^ parity(i)) == h for i in edges]
    give = [(i + 1) * chunk - jnp.where(own, REACH, 0) for i, own in zip(edges, owns)]
    take = [(i + 1) * chunk - jnp.where(own, 0, REACH) for i, own in zip(edges, owns)]
    reach_rows = REACH * rows

    half_pairs = chunk // 2
    pool = {
        "rhs": (rhs, chunk * rows, 0),
        "source": (source_t, chunk, 0),
        "source_blocks": (source_values, half_pairs, 1),
        "target": (target_t, chunk, 0),
        "target_blocks": (target_values, half_pairs, 1),
        "near": (near_t, chunk, 0),
    }
    arrays = {name: entry[0] for name, entry in pool.items()}
    queue = [(name, s) for s in range(steps) for name in ("source", "rhs", "source_blocks")]
    for s in range(steps):
        queue += [(name, s) for name in ("target_blocks", "target", "near")] + ([] if s else ["edges"])
    received = {}
    for entry in queue:
        if entry == "edges":
            piece = jnp.concatenate(
                [lax.dynamic_slice_in_dim(arrays["near"], g, REACH, 0) for g in give], axis=0
            )
        else:
            name, s = entry
            piece = cut(arrays[name], others[s], pool[name][1], pool[name][2])
        piece, arrays = lax.optimization_barrier((piece, arrays))
        received[entry] = swap(piece)

    peer_rhs = jnp.zeros(((box_count + 2 * REACH) * rows, columns), rhs.dtype)
    for s in range(steps):
        peer_rhs = lax.dynamic_update_slice_in_dim(
            peer_rhs, received["rhs", s], mine[s] * (chunk * rows) + reach_rows, 0
        )
    peer_tail = peer_rhs[box_count * rows : box_count * rows + reach_rows]
    peer_head = peer_rhs[reach_rows : 2 * reach_rows]
    up = [(i, i + 1) for i in range(leafs - 1)]
    down = [(i + 1, i) for i in range(leafs - 1)]
    tail = rhs[-reach_rows:]
    head = rhs[:reach_rows]

    def side(device):
        return parity(device >> bits)

    def same_side(other):
        return (sum((((other >> bits) >> k) & 1) for k in range(chunks.bit_length())) & 1) == home_parity

    both = ("leaf", "rhs")
    low_peer = lax.ppermute(
        jnp.where(same_side(d + 1), peer_tail, tail), both,
        [(2 * a + side(a), 2 * b + side(b)) for a, b in up],
    )
    high_peer = lax.ppermute(
        jnp.where(same_side(d - 1), peer_head, head), both,
        [(2 * a + side(a), 2 * b + side(b)) for a, b in down],
    )
    peer_rhs = lax.dynamic_update_slice_in_dim(peer_rhs, low_peer, 0, 0)
    peer_rhs = lax.dynamic_update_slice_in_dim(peer_rhs, high_peer, box_count * rows + reach_rows, 0)
    own_rhs = jnp.concatenate(
        [lax.ppermute(tail, "leaf", up), rhs, lax.ppermute(head, "leaf", down)], axis=0
    )

    params = pltpu.CompilerParams(
        dimension_semantics=("arbitrary",), vmem_limit_bytes=56 * 2**20
    )
    pair_count = group // 2
    wide = 2 * columns
    blocks_own = pl.BlockSpec(
        (levels, pair_count, 2, 2, half, rank), lambda t, i, *_: (0, i[0] * 2 + t, 0, 0, 0, 0)
    )
    blocks_peer = pl.BlockSpec((levels, pair_count, 2, 2, half, rank), lambda t, *_: (0, t, 0, 0, 0, 0))
    scale_spec = pl.BlockSpec(
        (levels, pair_count, 2, 2, rank), lambda t, i, *_: (0, i[0] * 2 + t, 0, 0, 0)
    )
    basis_own = pl.BlockSpec((group, half, rows), lambda t, i, *_: (i[0] * 2 + t, 0, 0))
    basis_peer = pl.BlockSpec((group, half, rows), lambda t, *_: (t, 0, 0))
    near_own = pl.BlockSpec((group, near_count, half, rows), lambda t, i, *_: (i[0] * 2 + t, 0, 0, 0))
    near_peer = pl.BlockSpec((group, near_count, half, rows), lambda t, *_: (t, 0, 0, 0))
    state_spec = pl.BlockSpec((group, rank, wide), lambda t, *_: (t, 0, 0))
    rhs_own = pl.BlockSpec((group * rows, columns), lambda t, i, *_: (i[0] * 2 + t, 0))
    rhs_peer = pl.BlockSpec((group * rows, columns), lambda t, *_: (t, 0))
    window_rows = (chunk + 2 * REACH) * rows
    window = pl.BlockSpec((window_rows, columns), lambda t, *_: (0, 0))
    weight_scratch = pltpu.VMEM((pair_count, 2 * rank, 2 * rank), rhs.dtype)
    state_scratch = pltpu.VMEM((group * rank, wide), rhs.dtype)

    rows_in = []
    for s in range(steps):
        index = jnp.stack([mine[s], h]).astype(jnp.int32)
        mixed = pl.pallas_call(
            source_kernel,
            out_shape=jax.ShapeDtypeStruct((chunk, rank, wide), rhs.dtype),
            grid_spec=pltpu.PrefetchScalarGridSpec(
                num_scalar_prefetch=1,
                grid=(2,),
                in_specs=[rhs_own, rhs_peer, basis_own, basis_peer, blocks_own, blocks_peer, scale_spec],
                out_specs=state_spec,
                scratch_shapes=[weight_scratch, state_scratch],
            ),
            compiler_params=params,
        )(index, rhs, received["rhs", s], source_t, received["source", s], source_values, received["source_blocks", s], source_scales)
        arrived = jnp.zeros((chunk, rank, wide), rhs.dtype)
        for k in range(span):
            slot = (d ^ k) & (span - 1)
            pairs = [
                (2 * a + e, 2 * (a ^ ((masks[e][s] << bits) | k)) + e) for a in range(leafs) for e in range(2)
            ]
            piece = lax.ppermute(cut(mixed, slot, quota), both, pairs)
            arrived = lax.dynamic_update_slice_in_dim(arrived, piece, slot * quota, 0)
        rows_in.append(arrived)

    offsets = near_offsets.reshape(-1)
    product = None
    returned = []
    for s in range(steps):
        index = jnp.stack([mine[s], h]).astype(jnp.int32)
        start = mine[s] * (chunk * rows)
        operands = [
            index, offsets, rows_in[s], target_values, received["target_blocks", s], target_scales,
            target_t, received["target", s], near_t, received["near", s],
            lax.dynamic_slice_in_dim(own_rhs, start, window_rows, 0),
            lax.dynamic_slice_in_dim(peer_rhs, start, window_rows, 0),
        ]
        specs = [
            state_spec, blocks_own, blocks_peer, scale_spec, basis_own, basis_peer, near_own, near_peer,
            window, window,
        ]
        aliases = {}
        if s:
            aliases = {len(operands): 0}
            operands.append(product)
            specs.append(pl.BlockSpec(memory_space=pl.ANY))
        far = pl.pallas_call(
            functools.partial(target_kernel, first=s == 0),
            out_shape=(
                jax.ShapeDtypeStruct((box_count * rows, columns), rhs.dtype),
                jax.ShapeDtypeStruct((chunk * rows, columns), rhs.dtype),
            ),
            grid_spec=pltpu.PrefetchScalarGridSpec(
                num_scalar_prefetch=2,
                grid=(2,),
                in_specs=specs,
                out_specs=(rhs_own, rhs_peer),
                scratch_shapes=[
                    weight_scratch,
                    state_scratch,
                    pltpu.VMEM((group, (near_count + 1) * 2 * half, rows), rhs.dtype),
                ],
            ),
            input_output_aliases=aliases,
            compiler_params=params,
        )
        product, send = far(*operands)
        at = others[s] * (chunk * rows)
        most = chunk * rows if s < steps - 1 else chunk * rows * 3 // 4
        for a, b in ((0, most), (most, chunk * rows)):
            if a < b:
                returned.append((swap(send[a:b]), at, a, b))

    row_box = jnp.concatenate([t + jnp.arange(REACH, dtype=jnp.int32) for t in take])
    edge_box = jnp.repeat(jnp.array([(i + 1) * chunk for i in edges], jnp.int32), REACH)
    below = jnp.repeat(jnp.stack(owns), REACH)
    read_box = row_box + jnp.concatenate(
        [lax.dynamic_slice_in_dim(near_offsets, t, REACH, 0) for t in take]
    ).T
    reads = jnp.where(below, read_box < edge_box, read_box >= edge_box)
    meta = jnp.concatenate(
        [h[None].astype(jnp.int32), row_box, jnp.where(reads, read_box, edge_box).reshape(-1),
         reads.astype(jnp.int32).reshape(-1)]
    )
    count = len(edges) * REACH

    def read_spec(k):
        return pl.BlockSpec((rows, columns), lambda j, m: (m[1 + (k + 1) * count + j], 0))

    at_edges = pl.pallas_call(
        edge_kernel,
        out_shape=jax.ShapeDtypeStruct((count * rows, columns), jnp.float32),
        grid_spec=pltpu.PrefetchScalarGridSpec(
            num_scalar_prefetch=1,
            grid=(count,),
            in_specs=[
                pl.BlockSpec((1, near_count, half, rows), lambda j, m: (m[1 + j], 0, 0, 0)),
                pl.BlockSpec((1, near_count, half, rows), lambda j, m: (j, 0, 0, 0)),
                *[read_spec(k) for k in range(near_count)],
            ],
            out_specs=pl.BlockSpec((rows, columns), lambda j, m: (j, 0)),
        ),
        compiler_params=params,
        name="edge_products",
    )(meta, near_t, received["edges"], *[rhs] * near_count)
    added = []
    for s in range(steps):
        products = cut(at_edges, others[s] >> 1, reach_rows)
        place = jnp.where(others[s] & 1, 0, (chunk - REACH) * rows)
        added.append(
            lax.dynamic_update_slice_in_dim(
                jnp.zeros((chunk * rows, columns), jnp.float32), products, place, 0
            )
        )
    for s, (part, at, a, b) in zip([*range(steps), steps - 1], returned):
        part = (part.astype(jnp.float32) + added[s][a:b]).astype(rhs.dtype)
        product = lax.dynamic_update_slice_in_dim(product, part, at + a, 0)
    return product


def solution(mesh):
    placed = (
        P("leaf", "rhs"),
        P("leaf", None, "rhs"),
        P("leaf", None, "rhs"),
        P("leaf", None, None, "rhs"),
        P("leaf", None),
        P(None, "leaf", None, None, "rhs", None),
        P(None, "leaf", None, None, None),
        P(None, "leaf", None, None, "rhs", None),
        P(None, "leaf", None, None, None),
    )
    return jax.shard_map(
        on_device, mesh=mesh, in_specs=placed, out_specs=P("leaf", "rhs"), check_vma=False
    )
```

profile of v0, /device:TPU:0, one launch (start us, length us, event | category | flops | bytes accessed | tf_op | source)
XLA Modules:
  0.0 367.4 jit_solution(9858901407492234010)
XLA Ops:
  0.0 1.7 dynamic-slice_bitcast_fusion
  1.7 2.3 constant_dynamic-slice_fusion.26
  3.9 3.0 collective-permute-start.12
  6.9 2.8 constant_dynamic-slice_fusion.25
  9.7 1.7 constant_dynamic-slice_fusion.24
  11.4 2.2 constant_dynamic-slice_fusion.23
  13.6 2.0 collective-permute-start.16
  15.7 2.8 constant_dynamic-slice_fusion.22
  18.5 2.0 collective-permute-start.2
  20.5 2.8 constant_dynamic-slice_fusion.17
  24.1 0.8 constant_dynamic-slice_fusion.15
  25.6 2.9 constant_dynamic-slice_fusion.12
  30.4 0.9 constant_dynamic-slice_fusion.10
  31.6 1.3 constant_dynamic-update-slice_fusion.7
  32.9 20.8 %collective-permute-done.rhs_peer = bf16[2048,256]{1,0:T(8,128)(2,1)} collective-permute-done((bf16[2048,256]{1,0:T(8,128)(2,1)}, bf16[2048,256]{1,0:T(8,128)(2,1)}, u32[]{:S(2)}, u32[]{:S(2)}) %collective-permute-start) | collective-permute-done | bytes 1048608 | tf_op jit(solution)/shard_map/ppermute | solution.py:180
  53.7 1.3 constant_dynamic-update-slice_fusion.6
  55.0 2.1 copy-done.1
  57.1 1.0 slice_select_fusion
  58.1 1.3 collective-permute-start.10
  60.7 4.6 %collective-permute-start.13 = (bf16[256,256]{1,0:T(8,128)(2,1)S(1)}, bf16[256,256]{1,0:T(8,128)(2,1)S(1)}, u32[]{:S(2)}, u32[]{:S(2)}) collective-permute-start(bf16[256,256]{1,0:T(8,128)(2,1)S(1)} %get-tuple-element.132), channel_id=1, source_target_pairs={{0,2},{2,4},{4,6},{6,9},{9,11},{11,13},{13,15},{15,17},{17,19},{19... | collective-permute-start | bytes 393224 | tf_op jit(solution)/shard_map/ppermute | solution.py:233
  65.3 1.3 collective-permute-start.14
  66.6 2.6 constant_dynamic-update-slice_fusion.13
  70.1 1.4 collective-permute-start.23
  71.5 21.6 %collective-permute-done.15.basis_peer = bf16[16,64,128]{2,1,0:T(8,128)(2,1)} collective-permute-done((bf16[16,64,128]{2,1,0:T(8,128)(2,1)}, bf16[16,64,128]{2,1,0:T(8,128)(2,1)}, u32[]{:S(2)}, u32[]{:S(2)}) %collective-permute-start.15) | collective-permute-done | bytes 262176 | tf_op jit(solution)/shard_map/ppermute | solution.py:180
  93.1 2.0 collective-permute-start.22
  95.1 1.6 constant_dynamic-slice_fusion.2
  96.7 6.8 %shard_map.101 = bf16[16,128,512]{2,1,0:T(8,128)(2,1)} custom-call(s32[2]{0:T(128)} %pad_add_fusion.2.idx, bf16[8192,256]{1,0:T(8,128)(2,1)} %rest_1_.1, bf16[2048,256]{1,0:T(8,128)(2,1)} %collective-permute-done.12.rhs_peer, bf16[64,64,128]{2,1,0:T(8,128)(2,1)} %bitcast.26, bf16[16,64,128]{2,1,0:T(8,128)(2,1)} %collective-permute-done.15.basis_peer, ...), custom_call_target="tpu_custom_call" | custom-call | tf_op jit(solution)/shard_map/pallas_call | solution.py:274
  103.5 73.7 %collective-permute-done.22.basis_peer = bf16[16,64,128]{2,1,0:T(8,128)(2,1)S(1)} collective-permute-done((bf16[16,64,128]{2,1,0:T(8,128)(2,1)S(1)}, bf16[16,64,128]{2,1,0:T(8,128)(2,1)S(1)}, u32[]{:S(2)}, u32[]{:S(2)}) %collective-permute-start.22) | collective-permute-done | bytes 262176 | tf_op jit(solution)/shard_map/ppermute | solution.py:180
  177.9 1.4 collective-permute-start.11
  179.4 2.9 constant_dynamic-slice_fusion.4
  182.2 6.1 %collective-permute-start.17 = (bf16[4,128,512]{2,1,0:T(8,128)(2,1)}, bf16[4,128,512]{2,1,0:T(8,128)(2,1)}, u32[]{:S(2)}, u32[]{:S(2)}) collective-permute-start(bf16[4,128,512]{2,1,0:T(8,128)(2,1)} %get-tuple-element.142), channel_id=1, source_target_pairs={{0,24},{1,17},{2,26},{3,19},{4,28},{5,21},{6,30},{7,23},{8,16},{9,... | collective-permute-start | bytes 1572872 | tf_op jit(solution)/shard_map/ppermute | solution.py:292
  188.5 1.4 collective-permute-start.18
  189.9 3.4 collective-permute-start.19
  193.3 1.7 constant_dynamic-slice_fusion.3
  195.0 6.9 %shard_map.100 = bf16[16,128,512]{2,1,0:T(8,128)(2,1)} custom-call(s32[2]{0:T(128)} %pad_add_fusion.1.idx, bf16[8192,256]{1,0:T(8,128)(2,1)} %rest_1_.1, bf16[2048,256]{1,0:T(8,128)(2,1)} %collective-permute-done.rhs_peer, bf16[64,64,128]{2,1,0:T(8,128)(2,1)} %bitcast.27, bf16[16,64,128]{2,1,0:T(8,128)(2,1)} %collective-permute-done.1.basis_peer, ...), custom_call_target="tpu_custom_call" | custom-call | tf_op jit(solution)/shard_map/pallas_call | solution.py:274
  202.0 1.7 collective-permute-start.20
  203.6 2.7 constant_dynamic-slice_fusion.18
  206.4 7.0 %collective-permute-done.18 = bf16[4,128,512]{2,1,0:T(8,128)(2,1)} collective-permute-done((bf16[4,128,512]{2,1,0:T(8,128)(2,1)}, bf16[4,128,512]{2,1,0:T(8,128)(2,1)}, u32[]{:S(2)}, u32[]{:S(2)}) %collective-permute-start.18) | collective-permute-done | bytes 524320 | tf_op jit(solution)/shard_map/ppermute | solution.py:292
  213.4 1.7 collective-permute-start.3
  215.1 10.1 %collective-permute-done.19 = bf16[4,128,512]{2,1,0:T(8,128)(2,1)} collective-permute-done((bf16[4,128,512]{2,1,0:T(8,128)(2,1)}, bf16[4,128,512]{2,1,0:T(8,128)(2,1)}, u32[]{:S(2)}, u32[]{:S(2)}) %collective-permute-start.19) | collective-permute-done | bytes 524320 | tf_op jit(solution)/shard_map/ppermute | solution.py:292
  225.4 1.1 constant_dynamic-update-slice_fusion.3
  226.5 1.1 constant_dynamic-update-slice_fusion.2
  227.6 1.1 constant_dynamic-update-slice_fusion.1
  228.7 6.7 %collective-permute-done.20 = bf16[4,128,512]{2,1,0:T(8,128)(2,1)S(1)} collective-permute-done((bf16[4,128,512]{2,1,0:T(8,128)(2,1)S(1)}, bf16[4,128,512]{2,1,0:T(8,128)(2,1)S(1)}, u32[]{:S(2)}, u32[]{:S(2)}) %collective-permute-start.20) | collective-permute-done | bytes 524320 | tf_op jit(solution)/shard_map/ppermute | solution.py:292
  235.4 1.3 collective-permute-start.5
  236.7 1.3 copy-done.2
  238.5 8.2 %shard_map.102 = (bf16[8192,256]{1,0:T(8,128)(2,1)}, bf16[2048,256]{1,0:T(8,128)(2,1)}) custom-call(s32[2]{0:T(128)} %pad_add_fusion.2.idx, s32[128]{0:T(128)} %reshape.18.offsets, bf16[16,128,512]{2,1,0:T(8,128)(2,1)} %copy-done.2, bf16[3,32,2,2,64,128]{5,4,3,2,1,0:T(8,128)(2,1)} %own.7, bf16[3,8,2,2,64,128]{5,4,3,2,1,0:T(8,128)(2,1)} %copy-done.6, ...), custom_call_target="tpu_custom_call" | custom-call | tf_op jit(solution)/shard_map/pallas_call | solution.py:337
  246.8 44.9 %collective-permute-start.24 = (bf16[2048,256]{1,0:T(8,128)(2,1)}, bf16[2048,256]{1,0:T(8,128)(2,1)S(1)}, u32[]{:S(2)}, u32[]{:S(2)}) collective-permute-start(bf16[2048,256]{1,0:T(8,128)(2,1)} %get-tuple-element.126), channel_id=1, source_target_pairs={{0,1},{1,0},{2,3},{3,2},{4,5},{5,4},{6,7},{7,6},{8,9},{9,8},{10,11... | collective-permute-start | bytes 3145736 | tf_op jit(solution)/shard_map/ppermute | solution.py:180
  292.9 0.8 copy-done.11
  293.8 21.5 %collective-permute-start.8 = (bf16[16,64,128]{2,1,0:T(8,128)(2,1)}, bf16[16,64,128]{2,1,0:T(8,128)(2,1)S(1)}, u32[]{:S(2)}, u32[]{:S(2)}) collective-permute-start(bf16[16,64,128]{2,1,0:T(8,128)(2,1)} %constant_dynamic-slice_fusion.11), channel_id=1, source_target_pairs={{0,1},{1,0},{2,3},{3,2},{4,5},{5,4},{6,7},{7,6},{8,9},{9,8},{10,11... | collective-permute-start | bytes 786440 | tf_op jit(solution)/shard_map/ppermute | solution.py:180
  315.3 1.1 constant_dynamic-update-slice_fusion.10
  316.4 1.1 constant_dynamic-update-slice_fusion.9
  317.5 8.9 %collective-permute-start.25 = (bf16[4,2,64,128]{3,2,1,0:T(8,128)(2,1)}, bf16[4,2,64,128]{3,2,1,0:T(8,128)(2,1)S(1)}, u32[]{:S(2)}, u32[]{:S(2)}) collective-permute-start(bf16[4,2,64,128]{3,2,1,0:T(8,128)(2,1)} %pad_maximum_fusion), channel_id=1, source_target_pairs={{0,1},{1,0},{2,3},{3,2},{4,5},{5,4},{6,7},{7,6},{8,9},{9,8},{10,11... | collective-permute-start | bytes 393224 | tf_op jit(solution)/shard_map/ppermute | solution.py:180
  326.3 1.1 constant_dynamic-update-slice_fusion.8.mixed
  327.4 5.4 %collective-permute-done.8.basis_peer = bf16[16,64,128]{2,1,0:T(8,128)(2,1)S(1)} collective-permute-done((bf16[16,64,128]{2,1,0:T(8,128)(2,1)}, bf16[16,64,128]{2,1,0:T(8,128)(2,1)S(1)}, u32[]{:S(2)}, u32[]{:S(2)}) %collective-permute-start.8) | collective-permute-done | bytes 262176 | tf_op jit(solution)/shard_map/ppermute | solution.py:180
  333.5 8.1 %shard_map.103 = (bf16[8192,256]{1,0:T(8,128)(2,1)}, bf16[2048,256]{1,0:T(8,128)(2,1)}) custom-call(s32[2]{0:T(128)} %pad_add_fusion.1.idx, s32[128]{0:T(128)} %reshape.18.offsets, bf16[16,128,512]{2,1,0:T(8,128)(2,1)} %copy-done.3, bf16[3,32,2,2,64,128]{5,4,3,2,1,0:T(8,128)(2,1)} %own.7, ...), custom_call_target="tpu_custom_call", output_to_operand_aliasing={{0}: (12, {})} | custom-call | tf_op jit(solution)/shard_map/pallas_call | solution.py:337
  341.6 1.2 slice.28
  342.8 2.1 collective-permute-start.26
  346.5 4.2 %edge_products.1 = f32[512,256]{1,0:T(8,128)} custom-call(s32[21]{0:T(128)} %concatenate.20.meta, bf16[64,2,64,128]{3,2,1,0:T(8,128)(2,1)} %bitcast.19, bf16[4,2,64,128]{3,2,1,0:T(8,128)(2,1)} %copy-done.16, bf16[8192,256]{1,0:T(8,128)(2,1)} %rest_1_.1, bf16[8192,256]{1,0:T(8,128)(2,1)} %rest_1_.1), custom_call_target="tpu_custom_call" | custom-call | tf_op jit(solution)/shard_map/edge_products/pallas_call | solution.py:360
  350.7 1.0 slice.30
  352.8 1.1 convert_dynamic-update-slice_fusion
  353.8 9.5 %collective-permute-done.26 = bf16[1536,256]{1,0:T(8,128)(2,1)S(1)} collective-permute-done((bf16[1536,256]{1,0:T(8,128)(2,1)S(1)}, bf16[1536,256]{1,0:T(8,128)(2,1)S(1)}, u32[]{:S(2)}, u32[]{:S(2)}) %collective-permute-start.26) | collective-permute-done | bytes 786464 | tf_op jit(solution)/shard_map/ppermute | solution.py:180
  363.3 1.1 fusion.1
  364.4 2.2 collective-permute-done.27
  (102 shorter events, 12.6 us)
Async XLA Ops:
  3.9 27.3 %collective-permute-start.12 = (bf16[2048,256]{1,0:T(8,128)(2,1)}, bf16[2048,256]{1,0:T(8,128)(2,1)}, u32[]{:S(2)}, u32[]{:S(2)}) collective-permute-start(bf16[2048,256]{1,0:T(8,128)(2,1)} %constant_dynamic-slice_fusion.26), channel_id=1, source_target_pairs={{0,1},{1,0},{2,3},{3,2},{4,5},{5,4},{6,7},{7,6},{8,9},{9,8},{10,11... | collective-permute-start | bytes 3145736 | tf_op jit(solution)/shard_map/ppermute | solution.py:180
  13.6 40.1 %collective-permute-start = (bf16[2048,256]{1,0:T(8,128)(2,1)}, bf16[2048,256]{1,0:T(8,128)(2,1)}, u32[]{:S(2)}, u32[]{:S(2)}) collective-permute-start(bf16[2048,256]{1,0:T(8,128)(2,1)} %constant_dynamic-slice_fusion.23), channel_id=1, source_target_pairs={{0,1},{1,0},{2,3},{3,2},{4,5},{5,4},{6,7},{7,6},{8,9},{9,8},{10,11... | collective-permute-start | bytes 3145736 | tf_op jit(solution)/shard_map/ppermute | solution.py:180
  13.6 83.1 %collective-permute-start.16 = (bf16[3,8,2,2,64,128]{5,4,3,2,1,0:T(8,128)(2,1)}, bf16[3,8,2,2,64,128]{5,4,3,2,1,0:T(8,128)(2,1)}, u32[]{:S(2)}, u32[]{:S(2)}) collective-permute-start(bf16[3,8,2,2,64,128]{5,4,3,2,1,0:T(8,128)(2,1)} %constant_dynamic-slice_fusion.25), channel_id=1, source_target_pairs={{0,1},{1,0},{2,3},{3,2},{4,5},{5,4},{6,7},{7,6},{8,9},{9,8},{10,11... | collective-permute-start | bytes 4718600 | tf_op jit(solution)/shard_map/ppermute | solution.py:180
  15.7 77.4 %collective-permute-start.15 = (bf16[16,64,128]{2,1,0:T(8,128)(2,1)}, bf16[16,64,128]{2,1,0:T(8,128)(2,1)}, u32[]{:S(2)}, u32[]{:S(2)}) collective-permute-start(bf16[16,64,128]{2,1,0:T(8,128)(2,1)} %dynamic-slice_bitcast_fusion), channel_id=1, source_target_pairs={{0,1},{1,0},{2,3},{3,2},{4,5},{5,4},{6,7},{7,6},{8,9},{9,8},{10,11... | collective-permute-start | bytes 786440 | tf_op jit(solution)/shard_map/ppermute | solution.py:180
  18.5 4.8 %copy-start.4 = (bf16[64,128,64]{1,2,0:T(8,128)(2,1)S(1)}, bf16[64,128,64]{1,2,0:T(8,128)(2,1)}, u32[]{:S(2)}) copy-start(bf16[64,128,64]{1,2,0:T(8,128)(2,1)} %param.12) | copy-start | bytes 3145732
  18.5 5.6 %copy-start = (bf16[64,2,128,64]{2,3,1,0:T(8,128)(2,1)S(1)}, bf16[64,2,128,64]{2,3,1,0:T(8,128)(2,1)}, u32[]{:S(2)}) copy-start(bf16[64,2,128,64]{2,3,1,0:T(8,128)(2,1)} %param.13) | copy-start | bytes 6291460
  18.5 171.4 %collective-permute-start.2 = (bf16[3,8,2,2,64,128]{5,4,3,2,1,0:T(8,128)(2,1)}, bf16[3,8,2,2,64,128]{5,4,3,2,1,0:T(8,128)(2,1)}, u32[]{:S(2)}, u32[]{:S(2)}) collective-permute-start(bf16[3,8,2,2,64,128]{5,4,3,2,1,0:T(8,128)(2,1)} %constant_dynamic-slice_fusion.22), channel_id=1, source_target_pairs={{0,1},{1,0},{2,3},{3,2},{4,5},{5,4},{6,7},{7,6},{8,9},{9,8},{10,11... | collective-permute-start | bytes 4718600 | tf_op jit(solution)/shard_map/ppermute | solution.py:180
  32.9 26.6 %copy-start.17 = (s32[64,2]{0,1:T(2,128)S(1)}, s32[64,2]{0,1:T(2,128)}, u32[]{:S(2)}) copy-start(s32[64,2]{0,1:T(2,128)} %param.14) | copy-start | bytes 1540
  32.9 27.5 %copy-start.18 = (s32[2]{0:T(128)S(1)}, s32[2]{0:T(128)}, u32[]{:S(2)}) copy-start(s32[2]{0:T(128)} %constant.69.clone) | copy-start | bytes 28
  55.0 2.1 copy-start.1
  58.1 7.1 %collective-permute-start.10 = (bf16[256,256]{1,0:T(8,128)(2,1)S(1)}, bf16[256,256]{1,0:T(8,128)(2,1)S(1)}, u32[]{:S(2)}, u32[]{:S(2)}) collective-permute-start(bf16[256,256]{1,0:T(8,128)(2,1)S(1)} %get-tuple-element.138), channel_id=1, source_target_pairs={{0,2},{2,4},{4,6},{6,8},{8,10},{10,12},{12,14},{14,16},{16,18},{18... | collective-permute-start | bytes 393224 | tf_op jit(solution)/shard_map/ppermute | solution.py:244
  60.7 8.6 %collective-permute-start.13 = (bf16[256,256]{1,0:T(8,128)(2,1)S(1)}, bf16[256,256]{1,0:T(8,128)(2,1)S(1)}, u32[]{:S(2)}, u32[]{:S(2)}) collective-permute-start(bf16[256,256]{1,0:T(8,128)(2,1)S(1)} %get-tuple-element.132), channel_id=1, source_target_pairs={{0,2},{2,4},{4,6},{6,9},{9,11},{11,13},{13,15},{15,17},{17,19},{19... | collective-permute-start | bytes 393224 | tf_op jit(solution)/shard_map/ppermute | solution.py:233
  65.3 4.8 %collective-permute-start.14 = (bf16[256,256]{1,0:T(8,128)(2,1)S(1)}, bf16[256,256]{1,0:T(8,128)(2,1)S(1)}, u32[]{:S(2)}, u32[]{:S(2)}) collective-permute-start(bf16[256,256]{1,0:T(8,128)(2,1)S(1)} %get-tuple-element.131), channel_id=1, source_target_pairs={{2,0},{4,2},{6,4},{9,6},{11,9},{13,11},{15,13},{17,15},{19,17},{21... | collective-permute-start | bytes 393224 | tf_op jit(solution)/shard_map/ppermute | solution.py:237
  66.6 3.5 slice-start
  66.6 3.4 slice-start.1
  66.6 26.4 %copy-start.15 = (bf16[16,64,128]{2,1,0:T(8,128)(2,1)S(1)}, bf16[16,64,128]{2,1,0:T(8,128)(2,1)}, u32[]{:S(2)}) copy-start(bf16[16,64,128]{2,1,0:T(8,128)(2,1)} %constant_dynamic-slice_fusion.16) | copy-start | bytes 786436
  69.3 167.4 %collective-permute-start.21 = (bf16[3,8,2,2,64,128]{5,4,3,2,1,0:T(8,128)(2,1)}, bf16[3,8,2,2,64,128]{5,4,3,2,1,0:T(8,128)(2,1)S(1)}, u32[]{:S(2)}, u32[]{:S(2)}) collective-permute-start(bf16[3,8,2,2,64,128]{5,4,3,2,1,0:T(8,128)(2,1)} %constant_dynamic-slice_fusion.17), channel_id=1, source_target_pairs={{0,1},{1,0},{2,3},{3,2},{4,5},{5,4},{6,7},{7,6},{8,9},{9,8},{10,11... | collective-permute-start | bytes 4718600 | tf_op jit(solution)/shard_map/ppermute | solution.py:180
  70.1 118.4 %collective-permute-start.23 = (bf16[16,2,64,128]{3,2,1,0:T(8,128)(2,1)}, bf16[16,2,64,128]{3,2,1,0:T(8,128)(2,1)S(1)}, u32[]{:S(2)}, u32[]{:S(2)}) collective-permute-start(bf16[16,2,64,128]{3,2,1,0:T(8,128)(2,1)} %constant_dynamic-slice_fusion.15), channel_id=1, source_target_pairs={{0,1},{1,0},{2,3},{3,2},{4,5},{5,4},{6,7},{7,6},{8,9},{9,8},{10,11... | collective-permute-start | bytes 1572872 | tf_op jit(solution)/shard_map/ppermute | solution.py:180
  93.1 84.2 %collective-permute-start.22 = (bf16[16,64,128]{2,1,0:T(8,128)(2,1)S(1)}, bf16[16,64,128]{2,1,0:T(8,128)(2,1)S(1)}, u32[]{:S(2)}, u32[]{:S(2)}) collective-permute-start(bf16[16,64,128]{2,1,0:T(8,128)(2,1)S(1)} %copy-done.15), channel_id=1, source_target_pairs={{0,1},{1,0},{2,3},{3,2},{4,5},{5,4},{6,7},{7,6},{8,9},{9,8},{10,11... | collective-permute-start | bytes 786440 | tf_op jit(solution)/shard_map/ppermute | solution.py:180
  96.7 91.7 %collective-permute-start.1 = (bf16[16,64,128]{2,1,0:T(8,128)(2,1)}, bf16[16,64,128]{2,1,0:T(8,128)(2,1)}, u32[]{:S(2)}, u32[]{:S(2)}) collective-permute-start(bf16[16,64,128]{2,1,0:T(8,128)(2,1)} %constant_dynamic-slice_fusion.24), channel_id=1, source_target_pairs={{0,1},{1,0},{2,3},{3,2},{4,5},{5,4},{6,7},{7,6},{8,9},{9,8},{10,11... | collective-permute-start | bytes 786440 | tf_op jit(solution)/shard_map/ppermute | solution.py:180
  177.2 0.7 copy-start.13
  177.9 10.5 %copy-start.7 = (bf16[3,8,2,2,64,128]{5,4,3,2,1,0:T(8,128)(2,1)S(1)}, bf16[3,8,2,2,64,128]{5,4,3,2,1,0:T(8,128)(2,1)}, u32[]{:S(2)}) copy-start(bf16[3,8,2,2,64,128]{5,4,3,2,1,0:T(8,128)(2,1)} %constant_dynamic-slice_fusion.12) | copy-start | bytes 4718596
  177.9 4.3 %collective-permute-start.11 = (bf16[256,256]{1,0:T(8,128)(2,1)S(1)}, bf16[256,256]{1,0:T(8,128)(2,1)S(1)}, u32[]{:S(2)}, u32[]{:S(2)}) collective-permute-start(bf16[256,256]{1,0:T(8,128)(2,1)S(1)} %get-tuple-element.137), channel_id=1, source_target_pairs={{2,0},{4,2},{6,4},{8,6},{10,8},{12,10},{14,12},{16,14},{18,16},{20... | collective-permute-start | bytes 393224 | tf_op jit(solution)/shard_map/ppermute | solution.py:244
  182.2 19.7 %collective-permute-start.17 = (bf16[4,128,512]{2,1,0:T(8,128)(2,1)}, bf16[4,128,512]{2,1,0:T(8,128)(2,1)}, u32[]{:S(2)}, u32[]{:S(2)}) collective-permute-start(bf16[4,128,512]{2,1,0:T(8,128)(2,1)} %get-tuple-element.142), channel_id=1, source_target_pairs={{0,24},{1,17},{2,26},{3,19},{4,28},{5,21},{6,30},{7,23},{8,16},{9,... | collective-permute-start | bytes 1572872 | tf_op jit(solution)/shard_map/ppermute | solution.py:292
  188.4 144.4 %collective-permute-start.7 = (bf16[3,8,2,2,64,128]{5,4,3,2,1,0:T(8,128)(2,1)S(1)}, bf16[3,8,2,2,64,128]{5,4,3,2,1,0:T(8,128)(2,1)}, u32[]{:S(2)}, u32[]{:S(2)}) collective-permute-start(bf16[3,8,2,2,64,128]{5,4,3,2,1,0:T(8,128)(2,1)S(1)} %copy-done.7), channel_id=1, source_target_pairs={{0,1},{1,0},{2,3},{3,2},{4,5},{5,4},{6,7},{7,6},{8,9},{9,8},{10,11... | collective-permute-start | bytes 4718600 | tf_op jit(solution)/shard_map/ppermute | solution.py:180
  188.5 6.5 %copy-start.8 = (bf16[16,2,64,128]{3,2,1,0:T(8,128)(2,1)}, bf16[16,2,64,128]{3,2,1,0:T(8,128)(2,1)S(1)}, u32[]{:S(2)}) copy-start(bf16[16,2,64,128]{3,2,1,0:T(8,128)(2,1)S(1)} %collective-permute-done.23.near_peer) | copy-start | bytes 1572868
  188.5 24.9 %collective-permute-start.18 = (bf16[4,128,512]{2,1,0:T(8,128)(2,1)}, bf16[4,128,512]{2,1,0:T(8,128)(2,1)}, u32[]{:S(2)}, u32[]{:S(2)}) collective-permute-start(bf16[4,128,512]{2,1,0:T(8,128)(2,1)} %get-tuple-element.141), channel_id=1, source_target_pairs={{0,26},{1,19},{2,24},{3,17},{4,30},{5,23},{6,28},{7,21},{8,18},{9,... | collective-permute-start | bytes 1572872 | tf_op jit(solution)/shard_map/ppermute | solution.py:292
  189.9 35.3 %collective-permute-start.19 = (bf16[4,128,512]{2,1,0:T(8,128)(2,1)}, bf16[4,128,512]{2,1,0:T(8,128)(2,1)}, u32[]{:S(2)}, u32[]{:S(2)}) collective-permute-start(bf16[4,128,512]{2,1,0:T(8,128)(2,1)} %get-tuple-element.140), channel_id=1, source_target_pairs={{0,28},{1,21},{2,30},{3,23},{4,24},{5,17},{6,26},{7,19},{8,20},{9,... | collective-permute-start | bytes 1572872 | tf_op jit(solution)/shard_map/ppermute | solution.py:292
  195.0 6.9 %copy-start.12 = (bf16[4,128,512]{2,1,0:T(8,128)(2,1)S(1)}, bf16[4,128,512]{2,1,0:T(8,128)(2,1)}, u32[]{:S(2)}) copy-start(bf16[4,128,512]{2,1,0:T(8,128)(2,1)} %get-tuple-element.139) | copy-start | bytes 1572868
  202.0 33.4 %collective-permute-start.20 = (bf16[4,128,512]{2,1,0:T(8,128)(2,1)S(1)}, bf16[4,128,512]{2,1,0:T(8,128)(2,1)S(1)}, u32[]{:S(2)}, u32[]{:S(2)}) collective-permute-start(bf16[4,128,512]{2,1,0:T(8,128)(2,1)S(1)} %copy-done.12), channel_id=1, source_target_pairs={{0,30},{1,23},{2,28},{3,21},{4,26},{5,19},{6,24},{7,17},{8,22},{9,... | collective-permute-start | bytes 1572872 | tf_op jit(solution)/shard_map/ppermute | solution.py:292
  213.4 78.4 %collective-permute-start.3 = (bf16[4,128,512]{2,1,0:T(8,128)(2,1)}, bf16[4,128,512]{2,1,0:T(8,128)(2,1)S(1)}, u32[]{:S(2)}, u32[]{:S(2)}) collective-permute-start(bf16[4,128,512]{2,1,0:T(8,128)(2,1)} %get-tuple-element.148), channel_id=1, source_target_pairs={{0,0},{1,9},{2,2},{3,11},{4,4},{5,13},{6,6},{7,15},{8,8},{9,1},{10... | collective-permute-start | bytes 1572872 | tf_op jit(solution)/shard_map/ppermute | solution.py:292
  225.2 67.4 %collective-permute-start.4 = (bf16[4,128,512]{2,1,0:T(8,128)(2,1)S(1)}, bf16[4,128,512]{2,1,0:T(8,128)(2,1)}, u32[]{:S(2)}, u32[]{:S(2)}) collective-permute-start(bf16[4,128,512]{2,1,0:T(8,128)(2,1)S(1)} %get-tuple-element.147), channel_id=1, source_target_pairs={{0,2},{1,11},{2,0},{3,9},{4,6},{5,15},{6,4},{7,13},{8,10},{9,3},{1... | collective-permute-start | bytes 1572872 | tf_op jit(solution)/shard_map/ppermute | solution.py:292
  235.4 58.4 %collective-permute-start.5 = (bf16[4,128,512]{2,1,0:T(8,128)(2,1)}, bf16[4,128,512]{2,1,0:T(8,128)(2,1)}, u32[]{:S(2)}, u32[]{:S(2)}) collective-permute-start(bf16[4,128,512]{2,1,0:T(8,128)(2,1)} %get-tuple-element.146), channel_id=1, source_target_pairs={{0,4},{1,13},{2,6},{3,15},{4,0},{5,9},{6,2},{7,11},{8,12},{9,5},{1... | collective-permute-start | bytes 1572872 | tf_op jit(solution)/shard_map/ppermute | solution.py:292
  236.7 1.4 copy-start.2
  236.7 1.8 copy-start.6
  238.5 53.3 %copy-start.9 = (bf16[16,2,64,128]{3,2,1,0:T(8,128)(2,1)S(1)}, bf16[16,2,64,128]{3,2,1,0:T(8,128)(2,1)}, u32[]{:S(2)}) copy-start(bf16[16,2,64,128]{3,2,1,0:T(8,128)(2,1)} %constant_dynamic-slice_fusion.10) | copy-start | bytes 1572868
  246.8 105.1 %collective-permute-start.24 = (bf16[2048,256]{1,0:T(8,128)(2,1)}, bf16[2048,256]{1,0:T(8,128)(2,1)S(1)}, u32[]{:S(2)}, u32[]{:S(2)}) collective-permute-start(bf16[2048,256]{1,0:T(8,128)(2,1)} %get-tuple-element.126), channel_id=1, source_target_pairs={{0,1},{1,0},{2,3},{3,2},{4,5},{5,4},{6,7},{7,6},{8,9},{9,8},{10,11... | collective-permute-start | bytes 3145736 | tf_op jit(solution)/shard_map/ppermute | solution.py:180
  291.8 0.8 copy-start.10
  291.8 41.0 %collective-permute-start.9 = (bf16[16,2,64,128]{3,2,1,0:T(8,128)(2,1)S(1)}, bf16[16,2,64,128]{3,2,1,0:T(8,128)(2,1)}, u32[]{:S(2)}, u32[]{:S(2)}) collective-permute-start(bf16[16,2,64,128]{3,2,1,0:T(8,128)(2,1)S(1)} %copy-done.9), channel_id=1, source_target_pairs={{0,1},{1,0},{2,3},{3,2},{4,5},{5,4},{6,7},{7,6},{8,9},{9,8},{10,11... | collective-permute-start | bytes 1572872 | tf_op jit(solution)/shard_map/ppermute | solution.py:180
  292.6 24.9 %collective-permute-start.6 = (bf16[4,128,512]{2,1,0:T(8,128)(2,1)}, bf16[4,128,512]{2,1,0:T(8,128)(2,1)}, u32[]{:S(2)}, u32[]{:S(2)}) collective-permute-start(bf16[4,128,512]{2,1,0:T(8,128)(2,1)} %get-tuple-element.145), channel_id=1, source_target_pairs={{0,6},{1,15},{2,4},{3,13},{4,2},{5,11},{6,0},{7,9},{8,14},{9,7},{1... | collective-permute-start | bytes 1572872 | tf_op jit(solution)/shard_map/ppermute | solution.py:292
  292.7 1.0 copy-start.11
  293.8 39.0 %collective-permute-start.8 = (bf16[16,64,128]{2,1,0:T(8,128)(2,1)}, bf16[16,64,128]{2,1,0:T(8,128)(2,1)S(1)}, u32[]{:S(2)}, u32[]{:S(2)}) collective-permute-start(bf16[16,64,128]{2,1,0:T(8,128)(2,1)} %constant_dynamic-slice_fusion.11), channel_id=1, source_target_pairs={{0,1},{1,0},{2,3},{3,2},{4,5},{5,4},{6,7},{7,6},{8,9},{9,8},{10,11... | collective-permute-start | bytes 786440 | tf_op jit(solution)/shard_map/ppermute | solution.py:180
  317.5 28.4 %collective-permute-start.25 = (bf16[4,2,64,128]{3,2,1,0:T(8,128)(2,1)}, bf16[4,2,64,128]{3,2,1,0:T(8,128)(2,1)S(1)}, u32[]{:S(2)}, u32[]{:S(2)}) collective-permute-start(bf16[4,2,64,128]{3,2,1,0:T(8,128)(2,1)} %pad_maximum_fusion), channel_id=1, source_target_pairs={{0,1},{1,0},{2,3},{3,2},{4,5},{5,4},{6,7},{7,6},{8,9},{9,8},{10,11... | collective-permute-start | bytes 393224 | tf_op jit(solution)/shard_map/ppermute | solution.py:180
  327.4 5.4 %copy-start.3 = (bf16[16,128,512]{2,1,0:T(8,128)(2,1)}, bf16[16,128,512]{2,1,0:T(8,128)(2,1)S(1)}, u32[]{:S(2)}) copy-start(bf16[16,128,512]{2,1,0:T(8,128)(2,1)S(1)} %constant_dynamic-update-slice_fusion.8.mixed) | copy-start | bytes 6291460
  332.8 0.7 copy-start.14
  342.8 20.5 %collective-permute-start.26 = (bf16[1536,256]{1,0:T(8,128)(2,1)S(1)}, bf16[1536,256]{1,0:T(8,128)(2,1)S(1)}, u32[]{:S(2)}, u32[]{:S(2)}) collective-permute-start(bf16[1536,256]{1,0:T(8,128)(2,1)S(1)} %slice.28), channel_id=1, source_target_pairs={{0,1},{1,0},{2,3},{3,2},{4,5},{5,4},{6,7},{7,6},{8,9},{9,8},{10,11... | collective-permute-start | bytes 2359304 | tf_op jit(solution)/shard_map/ppermute | solution.py:180
  345.8 0.7 copy-start.16
  351.7 1.0 copy-start.5
  351.7 15.0 %collective-permute-start.27 = (bf16[512,256]{1,0:T(8,128)(2,1)S(1)}, bf16[512,256]{1,0:T(8,128)(2,1)S(1)}, u32[]{:S(2)}, u32[]{:S(2)}) collective-permute-start(bf16[512,256]{1,0:T(8,128)(2,1)S(1)} %slice.30), channel_id=1, source_target_pairs={{0,1},{1,0},{2,3},{3,2},{4,5},{5,4},{6,7},{7,6},{8,9},{9,8},{10,11... | collective-permute-start | bytes 786440 | tf_op jit(solution)/shard_map/ppermute | solution.py:180
where the time goes:
time: 369 us; the launch traced here: 367 us
  waiting for transfers between devices  157 us (43%)
  starting transfers between devices  112 us (30%)
  local copies, waits for them, and re-layouts  56.8 us (15%)
  Pallas kernels  34.3 us (9%)
  other arithmetic  6.41 us (2%)
    ppermute x16, waiting for transfers between devices, swap(): return lax.ppermute(array, 'rhs', SWAP)  133 us
    ppermute x16, starting transfers between devices, swap(): return lax.ppermute(array, 'rhs', SWAP)  88.3 us
    dynamic_slice x14, local copies, waits for them, and re-layouts, cut(): return lax.dynamic_slice_in_dim(array, at * size, size, axis)  27.9 us
    ppermute x8, waiting for transfers between devices, on_device(): piece = lax.ppermute(cut(mixed, slot, quota), both, pairs)  23.8 us
    pallas_call x2, Pallas kernels, on_device(): product, send = far(*operands)  16.4 us
    ppermute x8, starting transfers between devices, on_device(): piece = lax.ppermute(cut(mixed, slot, quota), both, pairs)  15.5 us
    pallas_call x2, Pallas kernels, on_device(): pl.pallas_call(source_kernel, out_shape=jax.ShapeDtypeStruct((chunk, rank...  13.7 us
    unnamed x45, local copies, waits for them, and re-layouts  11.4 us
  transfers between devices with their start and end apart: 28, of which 9 were waited for; matrix products, arithmetic and copies ran while one was open for 14% of the time, Pallas kernels for 9%

commit v1 on v0

--- a/solution.py
+++ b/solution.py
@@ -117,23 +117,11 @@
         send[here, :] = total[:, columns:]
 
 
-def edge_kernel(meta, near_own, near_peer, *rest):
-    *boxes, out = rest
-    half = near_own.shape[2]
-    count = pl.num_programs(0)
-    j = pl.program_id(0)
-    h = meta[0]
-    total = jnp.zeros(out.shape, jnp.float32)
-    for k, box in enumerate(boxes):
-        part = jnp.zeros(out.shape, jnp.float32)
-        for near, at in ((near_own, h * half), (near_peer, (1 - h) * half)):
-            part += lax.dot_general(
-                near[0, k], box[pl.ds(pl.multiple_of(at, half), half), :], (((0,), (0,)), ((), ())),
-                preferred_element_type=jnp.float32,
-            )
-        reads = meta[1 + count + (len(boxes) + k) * count + j]
-        total += jnp.where(reads > 0, part, 0.0)
-    out[...] = total
+def cut_kernel(array, out, sem, *, span, masks):
+    at = (lax.axis_index("leaf") // span) ^ jnp.where(lax.axis_index("rhs") == 0, masks[1], masks[0])
+    copy = pltpu.make_async_copy(array.at[pl.ds(at * out.shape[0], out.shape[0])], out, sem)
+    copy.start()
+    copy.wait()
 
 
 def on_device(
@@ -182,9 +170,22 @@
     edges = [i for i in range(chunks - 1) if parity(i) != parity(i + 1)]
     assert edges == list(range(0, chunks, 2))
     owns = [(home_parity ^ parity(i)) == h for i in edges]
-    give = [(i + 1) * chunk - jnp.where(own, REACH, 0) for i, own in zip(edges, owns)]
-    take = [(i + 1) * chunk - jnp.where(own, 0, REACH) for i, own in zip(edges, owns)]
+    edge_pairs = [(i, j) for i in range(REACH) for j in range(REACH - i)]
     reach_rows = REACH * rows
+
+    def edge_sums(near, mine_too):
+        sums = []
+        for i, own in zip(edges, owns):
+            left = own if mine_too else ~own
+            at = (i + 1) * chunk - jnp.where(left, REACH, 0)
+            blocks = lax.dynamic_slice_in_dim(near, at, REACH, 0).astype(jnp.float32)
+            offset = lax.dynamic_slice_in_dim(near_offsets, at, REACH, 0)
+            blocks = jnp.where(left, blocks[::-1], blocks)
+            offset = jnp.where(left, -offset[::-1], offset)
+            for row, source in edge_pairs:
+                reads = (offset[row] == -(row + source + 1))[:, None, None]
+                sums.append(jnp.sum(jnp.where(reads, blocks[row], 0.0), axis=0).astype(near.dtype))
+        return jnp.stack(sums)
 
     half_pairs = chunk // 2
     pool = {
@@ -198,16 +199,23 @@
     arrays = {name: entry[0] for name, entry in pool.items()}
     queue = [(name, s) for s in range(steps) for name in ("source", "rhs", "source_blocks")]
     for s in range(steps):
-        queue += [(name, s) for name in ("target_blocks", "target", "near")] + ([] if s else ["edges"])
+        queue += [(name, s) for name in ("target_blocks", "target", "near")]
+    queue += ["edges"]
+    first_cut = pl.pallas_call(
+        functools.partial(cut_kernel, span=span, masks=[masks[0][0], masks[1][0]]),
+        out_shape=pltpu.VMEM((chunk, half, rows), rhs.dtype),
+        in_specs=[pl.BlockSpec(memory_space=pl.ANY)],
+        out_specs=pl.BlockSpec(memory_space=pltpu.VMEM),
+        scratch_shapes=[pltpu.SemaphoreType.DMA],
+        name="first_cut",
+    )
     received = {}
-    for entry in queue:
+    for n, entry in enumerate(queue):
         if entry == "edges":
-            piece = jnp.concatenate(
-                [lax.dynamic_slice_in_dim(arrays["near"], g, REACH, 0) for g in give], axis=0
-            )
+            piece = edge_sums(arrays["near"], True)
         else:
             name, s = entry
-            piece = cut(arrays[name], others[s], pool[name][1], pool[name][2])
+            piece = cut(arrays[name], others[s], pool[name][1], pool[name][2]) if n else first_cut(arrays[name])
         piece, arrays = lax.optimization_barrier((piece, arrays))
         received[entry] = swap(piece)
 
@@ -336,43 +344,31 @@
         )
         product, send = far(*operands)
         at = others[s] * (chunk * rows)
-        most = chunk * rows if s < steps - 1 else chunk * rows * 3 // 4
+        most = chunk * rows if s < steps - 1 else chunk * rows * 7 // 8
         for a, b in ((0, most), (most, chunk * rows)):
             if a < b:
                 returned.append((swap(send[a:b]), at, a, b))
 
-    row_box = jnp.concatenate([t + jnp.arange(REACH, dtype=jnp.int32) for t in take])
-    edge_box = jnp.repeat(jnp.array([(i + 1) * chunk for i in edges], jnp.int32), REACH)
-    below = jnp.repeat(jnp.stack(owns), REACH)
-    read_box = row_box + jnp.concatenate(
-        [lax.dynamic_slice_in_dim(near_offsets, t, REACH, 0) for t in take]
-    ).T
-    reads = jnp.where(below, read_box < edge_box, read_box >= edge_box)
-    meta = jnp.concatenate(
-        [h[None].astype(jnp.int32), row_box, jnp.where(reads, read_box, edge_box).reshape(-1),
-         reads.astype(jnp.int32).reshape(-1)]
-    )
-    count = len(edges) * REACH
-
-    def read_spec(k):
-        return pl.BlockSpec((rows, columns), lambda j, m: (m[1 + (k + 1) * count + j], 0))
-
-    at_edges = pl.pallas_call(
-        edge_kernel,
-        out_shape=jax.ShapeDtypeStruct((count * rows, columns), jnp.float32),
-        grid_spec=pltpu.PrefetchScalarGridSpec(
-            num_scalar_prefetch=1,
-            grid=(count,),
-            in_specs=[
-                pl.BlockSpec((1, near_count, half, rows), lambda j, m: (m[1 + j], 0, 0, 0)),
-                pl.BlockSpec((1, near_count, half, rows), lambda j, m: (j, 0, 0, 0)),
-                *[read_spec(k) for k in range(near_count)],
-            ],
-            out_specs=pl.BlockSpec((rows, columns), lambda j, m: (j, 0)),
-        ),
-        compiler_params=params,
-        name="edge_products",
-    )(meta, near_t, received["edges"], *[rhs] * near_count)
+    own_sums, peer_sums = edge_sums(near_t, False), received["edges"]
+    sums = jnp.where(
+        h == 0,
+        jnp.concatenate([own_sums, peer_sums], axis=1),
+        jnp.concatenate([peer_sums, own_sums], axis=1),
+    )
+    at_edges = []
+    for n, (i, own) in enumerate(zip(edges, owns)):
+        sources = lax.dynamic_slice_in_dim(rhs, ((i + 1) * chunk - jnp.where(own, REACH, 0)) * rows, reach_rows, 0)
+        sources = sources.reshape(REACH, rows, columns)
+        sources = jnp.where(own, sources[::-1], sources)
+        products = [jnp.zeros((rows, columns), jnp.float32) for _ in range(REACH)]
+        for p, (row, source) in enumerate(edge_pairs):
+            products[row] += lax.dot_general(
+                sums[n * len(edge_pairs) + p], sources[source], (((0,), (0,)), ((), ())),
+                preferred_element_type=jnp.float32,
+            )
+        products = jnp.stack(products)
+        at_edges.append(jnp.where(own, products, products[::-1]).reshape(reach_rows, columns))
+    at_edges = jnp.concatenate(at_edges, axis=0)
     added = []
     for s in range(steps):
         products = cut(at_edges, others[s] >> 1, reach_rows)

time: 369 us -> 376 us (1.019)
  waiting for transfers between devices: 157 us -> 172 us
  starting transfers between devices: 112 us -> 105 us
  local copies, waits for them, and re-layouts: 56.8 us -> 53 us
    ppermute x16, waiting for transfers between devices: 133 us -> 157 us  [swap(): return lax.ppermute(array, 'rhs', SWAP)]
    ppermute x8, waiting for transfers between devices: 23.8 us -> 15.9 us  [on_device(): piece = lax.ppermute(cut(mixed, slot, quota), both, pairs)]
    ppermute x16, starting transfers between devices: 88.3 us -> 83.9 us  [swap(): return lax.ppermute(array, 'rhs', SWAP)]
    unnamed x45 -> x55, local copies, waits for them, and re-layouts: 11.4 us -> 8.88 us
    dynamic_slice x14 -> x13, local copies, waits for them, and re-layouts: 27.9 us -> 26.6 us  [cut(): return lax.dynamic_slice_in_dim(array, at * size, size, axis)]
  transfers between devices with their start and end apart: 28 -> 28, of which waited for: 9 -> 9; matrix products, arithmetic and copies ran while one was open for 14% -> 10% of each run, Pallas kernels for 9% -> 8%
where the time goes in v1:
time: 376 us; the launch traced here: 375 us
  waiting for transfers between devices  172 us (46%)
  starting transfers between devices  105 us (28%)
  local copies, waits for them, and re-layouts  53 us (14%)
  Pallas kernels  31.1 us (8%)
  other arithmetic  9.44 us (3%)
    ppermute x16, waiting for transfers between devices, swap(): return lax.ppermute(array, 'rhs', SWAP)  157 us
    ppermute x16, starting transfers between devices, swap(): return lax.ppermute(array, 'rhs', SWAP)  83.9 us
    dynamic_slice x13, local copies, waits for them, and re-layouts, cut(): return lax.dynamic_slice_in_dim(array, at * size, size, axis)  26.6 us
    pallas_call x2, Pallas kernels, on_device(): product, send = far(*operands)  16.4 us
    ppermute x8, waiting for transfers between devices, on_device(): piece = lax.ppermute(cut(mixed, slot, quota), both, pairs)  15.9 us
    pallas_call x2, Pallas kernels, on_device(): pl.pallas_call(source_kernel, out_shape=jax.ShapeDtypeStruct((chunk, rank...  13.7 us
    ppermute x8, starting transfers between devices, on_device(): piece = lax.ppermute(cut(mixed, slot, quota), both, pairs)  13.1 us
    unnamed x55, local copies, waits for them, and re-layouts  8.88 us
  transfers between devices with their start and end apart: 28, of which 9 were waited for; matrix products, arithmetic and copies ran while one was open for 10% of the time, Pallas kernels for 8%

profile of v1, /device:TPU:0, one launch (start us, length us, event | category | flops | bytes accessed | tf_op | source)
XLA Modules:
  0.0 375.4 jit_solution(11523062154766224786)
XLA Ops:
  0.0 1.0 first_cut.1
  1.0 2.3 constant_dynamic-slice_fusion.28
  3.3 2.8 constant_dynamic-slice_fusion.27
  6.0 1.7 constant_dynamic-slice_fusion.26
  7.7 2.3 constant_dynamic-slice_fusion.25
  10.0 2.8 constant_dynamic-slice_fusion.24
  12.8 3.0 constant_dynamic-slice_fusion.19
  16.6 0.8 constant_dynamic-slice_fusion.17
  17.4 2.8 constant_dynamic-slice_fusion.16
  20.9 0.8 constant_dynamic-slice_fusion.14
  26.4 3.0 collective-permute-start.25
  29.4 2.0 collective-permute-start.12
  31.5 2.0 collective-permute-start.15
  34.4 1.0 reverse_select_fusion.6
  38.0 1.0 maximum_select_fusion
  39.0 39.2 %collective-permute-done.12.rhs_peer = bf16[2048,256]{1,0:T(8,128)(2,1)} collective-permute-done((bf16[2048,256]{1,0:T(8,128)(2,1)}, bf16[2048,256]{1,0:T(8,128)(2,1)}, u32[]{:S(2)}, u32[]{:S(2)}) %collective-permute-start.12) | collective-permute-done | bytes 1048608 | tf_op jit(solution)/shard_map/ppermute | solution.py:168
  78.5 1.5 constant_dynamic-update-slice_fusion.22
  80.1 1.1 copy-done
  82.7 1.3 collective-permute-start.10
  84.0 0.9 fusion.19
  84.9 4.6 %collective-permute-start.13 = (bf16[256,256]{1,0:T(8,128)(2,1)S(1)}, bf16[256,256]{1,0:T(8,128)(2,1)S(1)}, u32[]{:S(2)}, u32[]{:S(2)}) collective-permute-start(bf16[256,256]{1,0:T(8,128)(2,1)S(1)} %get-tuple-element.150), channel_id=1, source_target_pairs={{0,2},{2,4},{4,6},{6,9},{9,11},{11,13},{13,15},{15,17},{17,19},{19... | collective-permute-start | bytes 393224 | tf_op jit(solution)/shard_map/ppermute | solution.py:241
  89.5 1.3 collective-permute-start.14
  91.4 2.2 constant_dynamic-update-slice_fusion.1
  93.7 2.1 collective-permute-start.1
  95.8 21.8 %collective-permute-done.15.basis_peer = bf16[16,64,128]{2,1,0:T(8,128)(2,1)} collective-permute-done((bf16[16,64,128]{2,1,0:T(8,128)(2,1)S(1)}, bf16[16,64,128]{2,1,0:T(8,128)(2,1)}, u32[]{:S(2)}, u32[]{:S(2)}) %collective-permute-start.15) | collective-permute-done | bytes 262176 | tf_op jit(solution)/shard_map/ppermute | solution.py:168
  117.5 2.1 collective-permute-start.23
  119.7 1.3 collective-permute-start.11
  120.9 6.8 %shard_map.92 = bf16[16,128,512]{2,1,0:T(8,128)(2,1)} custom-call(s32[2]{0:T(128)} %pad_add_fusion.1.idx, bf16[8192,256]{1,0:T(8,128)(2,1)} %rhs_own.3, bf16[2048,256]{1,0:T(8,128)(2,1)} %collective-permute-done.12.rhs_peer, bf16[64,64,128]{2,1,0:T(8,128)(2,1)} %bitcast.133, bf16[16,64,128]{2,1,0:T(8,128)(2,1)} %collective-permute-done.15.basis_peer, ...), custom_call_target="tpu_custom_call" | custom-call | tf_op jit(solution)/shard_map/pallas_call | solution.py:282
  127.7 3.0 constant_dynamic-slice_fusion.8
  130.7 59.9 %collective-permute-done.1.basis_peer = bf16[16,64,128]{2,1,0:T(8,128)(2,1)} collective-permute-done((bf16[16,64,128]{2,1,0:T(8,128)(2,1)}, bf16[16,64,128]{2,1,0:T(8,128)(2,1)}, u32[]{:S(2)}, u32[]{:S(2)}) %collective-permute-start.1) | collective-permute-done | bytes 262176 | tf_op jit(solution)/shard_map/ppermute | solution.py:168
  190.6 2.1 collective-permute-start.22
  192.7 3.6 collective-permute-start.17
  196.3 1.8 constant_dynamic-slice_fusion.6
  198.0 1.5 constant_dynamic-update-slice_fusion
  199.6 6.9 %shard_map.91 = bf16[16,128,512]{2,1,0:T(8,128)(2,1)} custom-call(s32[2]{0:T(128)} %pad_add_fusion.idx, bf16[8192,256]{1,0:T(8,128)(2,1)} %rhs_own.3, bf16[2048,256]{1,0:T(8,128)(2,1)} %copy-done.5, bf16[64,64,128]{2,1,0:T(8,128)(2,1)} %bitcast.134, bf16[16,64,128]{2,1,0:T(8,128)(2,1)} %collective-permute-done.1.basis_peer, ...), custom_call_target="tpu_custom_call" | custom-call | tf_op jit(solution)/shard_map/pallas_call | solution.py:282
  206.6 4.9 %collective-permute-start.19 = (bf16[4,128,512]{2,1,0:T(8,128)(2,1)S(1)}, bf16[4,128,512]{2,1,0:T(8,128)(2,1)S(1)}, u32[]{:S(2)}, u32[]{:S(2)}) collective-permute-start(bf16[4,128,512]{2,1,0:T(8,128)(2,1)S(1)} %copy-done.15), channel_id=1, source_target_pairs={{0,28},{1,21},{2,30},{3,23},{4,24},{5,17},{6,26},{7,19},{8,20},{9,... | collective-permute-start | bytes 1572872 | tf_op jit(solution)/shard_map/ppermute | solution.py:300
  211.5 2.9 constant_dynamic-slice_fusion.20
  214.4 1.9 collective-permute-start.7
  216.3 3.9 %collective-permute-done.18 = bf16[4,128,512]{2,1,0:T(8,128)(2,1)} collective-permute-done((bf16[4,128,512]{2,1,0:T(8,128)(2,1)}, bf16[4,128,512]{2,1,0:T(8,128)(2,1)}, u32[]{:S(2)}, u32[]{:S(2)}) %collective-permute-start.18) | collective-permute-done | bytes 524320 | tf_op jit(solution)/shard_map/ppermute | solution.py:300
  220.2 1.7 collective-permute-start.3
  221.8 3.4 constant_dynamic-slice_fusion.7
  225.2 7.7 %collective-permute-done.19 = bf16[4,128,512]{2,1,0:T(8,128)(2,1)S(1)} collective-permute-done((bf16[4,128,512]{2,1,0:T(8,128)(2,1)S(1)}, bf16[4,128,512]{2,1,0:T(8,128)(2,1)S(1)}, u32[]{:S(2)}, u32[]{:S(2)}) %collective-permute-start.19) | collective-permute-done | bytes 524320 | tf_op jit(solution)/shard_map/ppermute | solution.py:300
  233.1 1.1 constant_dynamic-update-slice_fusion.18
  234.2 1.1 constant_dynamic-update-slice_fusion.17
  235.3 4.3 %collective-permute-done.20 = bf16[4,128,512]{2,1,0:T(8,128)(2,1)S(1)} collective-permute-done((bf16[4,128,512]{2,1,0:T(8,128)(2,1)S(1)}, bf16[4,128,512]{2,1,0:T(8,128)(2,1)S(1)}, u32[]{:S(2)}, u32[]{:S(2)}) %collective-permute-start.20) | collective-permute-done | bytes 524320 | tf_op jit(solution)/shard_map/ppermute | solution.py:300
  239.6 1.1 collective-permute-start.5
  240.8 1.8 collective-permute-start.6
  242.6 8.3 %shard_map.93 = (bf16[8192,256]{1,0:T(8,128)(2,1)}, bf16[2048,256]{1,0:T(8,128)(2,1)}) custom-call(s32[2]{0:T(128)} %pad_add_fusion.1.idx, s32[128]{0:T(128)} %reshape.195.offsets, bf16[16,128,512]{2,1,0:T(8,128)(2,1)} %copy-done.2, bf16[3,32,2,2,64,128]{5,4,3,2,1,0:T(8,128)(2,1)} %own.7, bf16[3,8,2,2,64,128]{5,4,3,2,1,0:T(8,128)(2,1)} %copy-done.6, ...), custom_call_target="tpu_custom_call" | custom-call | tf_op jit(solution)/shard_map/pallas_call | solution.py:345
  250.9 0.8 copy-done.12
  251.8 46.4 %collective-permute-start.24 = (bf16[2048,256]{1,0:T(8,128)(2,1)}, bf16[2048,256]{1,0:T(8,128)(2,1)S(1)}, u32[]{:S(2)}, u32[]{:S(2)}) collective-permute-start(bf16[2048,256]{1,0:T(8,128)(2,1)} %get-tuple-element.121), channel_id=1, source_target_pairs={{0,1},{1,0},{2,3},{3,2},{4,5},{5,4},{6,7},{7,6},{8,9},{9,8},{10,11... | collective-permute-start | bytes 3145736 | tf_op jit(solution)/shard_map/ppermute | solution.py:168
  298.2 1.0 fusion.2
  299.2 8.1 %collective-permute-start.9 = (bf16[16,2,64,128]{3,2,1,0:T(8,128)(2,1)S(1)}, bf16[16,2,64,128]{3,2,1,0:T(8,128)(2,1)S(1)}, u32[]{:S(2)}, u32[]{:S(2)}) collective-permute-start(bf16[16,2,64,128]{3,2,1,0:T(8,128)(2,1)S(1)} %copy-done.11), channel_id=1, source_target_pairs={{0,1},{1,0},{2,3},{3,2},{4,5},{5,4},{6,7},{7,6},{8,9},{9,8},{10,11... | collective-permute-start | bytes 1572872 | tf_op jit(solution)/shard_map/ppermute | solution.py:168
  307.2 0.9 convolution_bitcast_fusion.1
  308.5 12.0 %collective-permute-start.8 = (bf16[16,64,128]{2,1,0:T(8,128)(2,1)S(1)}, bf16[16,64,128]{2,1,0:T(8,128)(2,1)S(1)}, u32[]{:S(2)}, u32[]{:S(2)}) collective-permute-start(bf16[16,64,128]{2,1,0:T(8,128)(2,1)S(1)} %copy-done.19), channel_id=1, source_target_pairs={{0,1},{1,0},{2,3},{3,2},{4,5},{5,4},{6,7},{7,6},{8,9},{9,8},{10,11... | collective-permute-start | bytes 786440 | tf_op jit(solution)/shard_map/ppermute | solution.py:168
  320.4 1.1 constant_dynamic-update-slice_fusion.25
  321.5 1.1 constant_dynamic-update-slice_fusion.24
  322.7 16.5 %collective-permute-done.8.basis_peer = bf16[16,64,128]{2,1,0:T(8,128)(2,1)S(1)} collective-permute-done((bf16[16,64,128]{2,1,0:T(8,128)(2,1)S(1)}, bf16[16,64,128]{2,1,0:T(8,128)(2,1)S(1)}, u32[]{:S(2)}, u32[]{:S(2)}) %collective-permute-start.8) | collective-permute-done | bytes 262176 | tf_op jit(solution)/shard_map/ppermute | solution.py:168
  340.1 8.1 %shard_map.94 = (bf16[8192,256]{1,0:T(8,128)(2,1)}, bf16[2048,256]{1,0:T(8,128)(2,1)}) custom-call(s32[2]{0:T(128)} %pad_add_fusion.idx, s32[128]{0:T(128)} %reshape.195.offsets, bf16[16,128,512]{2,1,0:T(8,128)(2,1)} %copy-done.3, bf16[3,32,2,2,64,128]{5,4,3,2,1,0:T(8,128)(2,1)} %own.7, ...), custom_call_target="tpu_custom_call", output_to_operand_aliasing={{0}: (12, {})} | custom-call | tf_op jit(solution)/shard_map/pallas_call | solution.py:345
  348.2 1.2 slice.142
  349.5 1.9 collective-permute-start.26
  351.4 0.9 slice.144
  353.2 1.1 convert_dynamic-update-slice_fusion
  354.3 18.5 %collective-permute-done.26 = bf16[1792,256]{1,0:T(8,128)(2,1)S(1)} collective-permute-done((bf16[1792,256]{1,0:T(8,128)(2,1)S(1)}, bf16[1792,256]{1,0:T(8,128)(2,1)S(1)}, u32[]{:S(2)}, u32[]{:S(2)}) %collective-permute-start.26) | collective-permute-done | bytes 917536 | tf_op jit(solution)/shard_map/ppermute | solution.py:168
  372.8 1.2 fusion.3
  (131 shorter events, 15.9 us)
Async XLA Ops:
  12.8 3.0 copy-start.4
  12.8 3.7 copy-start.1
  17.4 4.4 %copy-start.20 = (s32[64,2]{0,1:T(2,128)S(1)}, s32[64,2]{0,1:T(2,128)}, u32[]{:S(2)}) copy-start(s32[64,2]{0,1:T(2,128)} %param.13) | copy-start | bytes 1540
  26.4 11.6 %collective-permute-start.25 = (bf16[6,64,128]{2,1,0:T(8,128)(2,1)}, bf16[6,64,128]{2,1,0:T(8,128)(2,1)}, u32[]{:S(2)}, u32[]{:S(2)}) collective-permute-start(bf16[6,64,128]{2,1,0:T(8,128)(2,1)} %constant_dynamic-update-slice_fusion.9), channel_id=1, source_target_pairs={{0,1},{1,0},{2,3},{3,2},{4,5},{5,4},{6,7},{7,6},{8,9},{9,8},{10,11... | collective-permute-start | bytes 294920 | tf_op jit(solution)/shard_map/ppermute | solution.py:168
  29.4 50.6 %collective-permute-start = (bf16[2048,256]{1,0:T(8,128)(2,1)}, bf16[2048,256]{1,0:T(8,128)(2,1)S(1)}, u32[]{:S(2)}, u32[]{:S(2)}) collective-permute-start(bf16[2048,256]{1,0:T(8,128)(2,1)} %constant_dynamic-slice_fusion.25), channel_id=1, source_target_pairs={{0,1},{1,0},{2,3},{3,2},{4,5},{5,4},{6,7},{7,6},{8,9},{9,8},{10,11... | collective-permute-start | bytes 3145736 | tf_op jit(solution)/shard_map/ppermute | solution.py:168
  29.4 48.8 %collective-permute-start.12 = (bf16[2048,256]{1,0:T(8,128)(2,1)}, bf16[2048,256]{1,0:T(8,128)(2,1)}, u32[]{:S(2)}, u32[]{:S(2)}) collective-permute-start(bf16[2048,256]{1,0:T(8,128)(2,1)} %constant_dynamic-slice_fusion.28), channel_id=1, source_target_pairs={{0,1},{1,0},{2,3},{3,2},{4,5},{5,4},{6,7},{7,6},{8,9},{9,8},{10,11... | collective-permute-start | bytes 3145736 | tf_op jit(solution)/shard_map/ppermute | solution.py:168
  31.4 88.2 %collective-permute-start.16 = (bf16[3,8,2,2,64,128]{5,4,3,2,1,0:T(8,128)(2,1)}, bf16[3,8,2,2,64,128]{5,4,3,2,1,0:T(8,128)(2,1)}, u32[]{:S(2)}, u32[]{:S(2)}) collective-permute-start(bf16[3,8,2,2,64,128]{5,4,3,2,1,0:T(8,128)(2,1)} %constant_dynamic-slice_fusion.27), channel_id=1, source_target_pairs={{0,1},{1,0},{2,3},{3,2},{4,5},{5,4},{6,7},{7,6},{8,9},{9,8},{10,11... | collective-permute-start | bytes 4718600 | tf_op jit(solution)/shard_map/ppermute | solution.py:168
  31.5 86.1 %collective-permute-start.15 = (bf16[16,64,128]{2,1,0:T(8,128)(2,1)S(1)}, bf16[16,64,128]{2,1,0:T(8,128)(2,1)}, u32[]{:S(2)}, u32[]{:S(2)}) collective-permute-start(bf16[16,64,128]{2,1,0:T(8,128)(2,1)S(1)} %first_cut.1), channel_id=1, source_target_pairs={{0,1},{1,0},{2,3},{3,2},{4,5},{5,4},{6,7},{7,6},{8,9},{9,8},{10,11... | collective-permute-start | bytes 786440 | tf_op jit(solution)/shard_map/ppermute | solution.py:168
  38.0 158.3 %collective-permute-start.2 = (bf16[3,8,2,2,64,128]{5,4,3,2,1,0:T(8,128)(2,1)}, bf16[3,8,2,2,64,128]{5,4,3,2,1,0:T(8,128)(2,1)}, u32[]{:S(2)}, u32[]{:S(2)}) collective-permute-start(bf16[3,8,2,2,64,128]{5,4,3,2,1,0:T(8,128)(2,1)} %constant_dynamic-slice_fusion.24), channel_id=1, source_target_pairs={{0,1},{1,0},{2,3},{3,2},{4,5},{5,4},{6,7},{7,6},{8,9},{9,8},{10,11... | collective-permute-start | bytes 4718600 | tf_op jit(solution)/shard_map/ppermute | solution.py:168
  39.0 45.0 %copy-start.9 = (bf16[6,128,128]{2,1,0:T(8,128)(2,1)}, bf16[6,128,128]{2,1,0:T(8,128)(2,1)S(1)}, u32[]{:S(2)}) copy-start(bf16[6,128,128]{2,1,0:T(8,128)(2,1)S(1)} %maximum_select_fusion) | copy-start | bytes 589828
  78.5 2.7 copy-start
  80.0 2.4 copy-start.5
  82.7 6.8 %collective-permute-start.10 = (bf16[256,256]{1,0:T(8,128)(2,1)S(1)}, bf16[256,256]{1,0:T(8,128)(2,1)S(1)}, u32[]{:S(2)}, u32[]{:S(2)}) collective-permute-start(bf16[256,256]{1,0:T(8,128)(2,1)S(1)} %get-tuple-element.158), channel_id=1, source_target_pairs={{0,2},{2,4},{4,6},{6,8},{8,10},{10,12},{12,14},{14,16},{16,18},{18... | collective-permute-start | bytes 393224 | tf_op jit(solution)/shard_map/ppermute | solution.py:252
  84.9 8.8 %collective-permute-start.13 = (bf16[256,256]{1,0:T(8,128)(2,1)S(1)}, bf16[256,256]{1,0:T(8,128)(2,1)S(1)}, u32[]{:S(2)}, u32[]{:S(2)}) collective-permute-start(bf16[256,256]{1,0:T(8,128)(2,1)S(1)} %get-tuple-element.150), channel_id=1, source_target_pairs={{0,2},{2,4},{4,6},{6,9},{9,11},{11,13},{13,15},{15,17},{17,19},{19... | collective-permute-start | bytes 393224 | tf_op jit(solution)/shard_map/ppermute | solution.py:241
  89.5 4.2 %collective-permute-start.14 = (bf16[256,256]{1,0:T(8,128)(2,1)S(1)}, bf16[256,256]{1,0:T(8,128)(2,1)S(1)}, u32[]{:S(2)}, u32[]{:S(2)}) collective-permute-start(bf16[256,256]{1,0:T(8,128)(2,1)S(1)} %get-tuple-element.149), channel_id=1, source_target_pairs={{2,0},{4,2},{6,4},{9,6},{11,9},{13,11},{15,13},{17,15},{19,17},{21... | collective-permute-start | bytes 393224 | tf_op jit(solution)/shard_map/ppermute | solution.py:245
  91.4 2.2 copy-start.8
  93.7 147.1 %collective-permute-start.21 = (bf16[3,8,2,2,64,128]{5,4,3,2,1,0:T(8,128)(2,1)S(1)}, bf16[3,8,2,2,64,128]{5,4,3,2,1,0:T(8,128)(2,1)S(1)}, u32[]{:S(2)}, u32[]{:S(2)}) collective-permute-start(bf16[3,8,2,2,64,128]{5,4,3,2,1,0:T(8,128)(2,1)S(1)} %copy-done.8), channel_id=1, source_target_pairs={{0,1},{1,0},{2,3},{3,2},{4,5},{5,4},{6,7},{7,6},{8,9},{9,8},{10,11... | collective-permute-start | bytes 4718600 | tf_op jit(solution)/shard_map/ppermute | solution.py:168
  93.7 96.9 %collective-permute-start.1 = (bf16[16,64,128]{2,1,0:T(8,128)(2,1)}, bf16[16,64,128]{2,1,0:T(8,128)(2,1)}, u32[]{:S(2)}, u32[]{:S(2)}) collective-permute-start(bf16[16,64,128]{2,1,0:T(8,128)(2,1)} %constant_dynamic-slice_fusion.26), channel_id=1, source_target_pairs={{0,1},{1,0},{2,3},{3,2},{4,5},{5,4},{6,7},{7,6},{8,9},{9,8},{10,11... | collective-permute-start | bytes 786440 | tf_op jit(solution)/shard_map/ppermute | solution.py:168
  117.5 96.8 %collective-permute-start.23 = (bf16[16,2,64,128]{3,2,1,0:T(8,128)(2,1)}, bf16[16,2,64,128]{3,2,1,0:T(8,128)(2,1)}, u32[]{:S(2)}, u32[]{:S(2)}) collective-permute-start(bf16[16,2,64,128]{3,2,1,0:T(8,128)(2,1)} %constant_dynamic-slice_fusion.17), channel_id=1, source_target_pairs={{0,1},{1,0},{2,3},{3,2},{4,5},{5,4},{6,7},{7,6},{8,9},{9,8},{10,11... | collective-permute-start | bytes 1572872 | tf_op jit(solution)/shard_map/ppermute | solution.py:168
  119.7 73.0 %collective-permute-start.11 = (bf16[256,256]{1,0:T(8,128)(2,1)}, bf16[256,256]{1,0:T(8,128)(2,1)}, u32[]{:S(2)}, u32[]{:S(2)}) collective-permute-start(bf16[256,256]{1,0:T(8,128)(2,1)} %get-tuple-element.157), channel_id=1, source_target_pairs={{2,0},{4,2},{6,4},{8,6},{10,8},{12,10},{14,12},{16,14},{18,16},{20... | collective-permute-start | bytes 393224 | tf_op jit(solution)/shard_map/ppermute | solution.py:252
  190.6 16.0 %collective-permute-start.22 = (bf16[16,64,128]{2,1,0:T(8,128)(2,1)}, bf16[16,64,128]{2,1,0:T(8,128)(2,1)S(1)}, u32[]{:S(2)}, u32[]{:S(2)}) collective-permute-start(bf16[16,64,128]{2,1,0:T(8,128)(2,1)} %constant_dynamic-slice_fusion.18), channel_id=1, source_target_pairs={{0,1},{1,0},{2,3},{3,2},{4,5},{5,4},{6,7},{7,6},{8,9},{9,8},{10,11... | collective-permute-start | bytes 786440 | tf_op jit(solution)/shard_map/ppermute | solution.py:168
  192.7 23.6 %collective-permute-start.17 = (bf16[4,128,512]{2,1,0:T(8,128)(2,1)}, bf16[4,128,512]{2,1,0:T(8,128)(2,1)}, u32[]{:S(2)}, u32[]{:S(2)}) collective-permute-start(bf16[4,128,512]{2,1,0:T(8,128)(2,1)} %get-tuple-element.166), channel_id=1, source_target_pairs={{0,24},{1,17},{2,26},{3,19},{4,28},{5,21},{6,30},{7,23},{8,16},{9,... | collective-permute-start | bytes 1572872 | tf_op jit(solution)/shard_map/ppermute | solution.py:300
  196.3 23.9 %collective-permute-start.18 = (bf16[4,128,512]{2,1,0:T(8,128)(2,1)}, bf16[4,128,512]{2,1,0:T(8,128)(2,1)}, u32[]{:S(2)}, u32[]{:S(2)}) collective-permute-start(bf16[4,128,512]{2,1,0:T(8,128)(2,1)} %get-tuple-element.165), channel_id=1, source_target_pairs={{0,26},{1,19},{2,24},{3,17},{4,30},{5,23},{6,28},{7,21},{8,18},{9,... | collective-permute-start | bytes 1572872 | tf_op jit(solution)/shard_map/ppermute | solution.py:300
  199.6 7.0 %copy-start.15 = (bf16[4,128,512]{2,1,0:T(8,128)(2,1)S(1)}, bf16[4,128,512]{2,1,0:T(8,128)(2,1)}, u32[]{:S(2)}) copy-start(bf16[4,128,512]{2,1,0:T(8,128)(2,1)} %get-tuple-element.164) | copy-start | bytes 1572868
  206.6 7.8 %copy-start.17 = (bf16[16,64,128]{2,1,0:T(8,128)(2,1)}, bf16[16,64,128]{2,1,0:T(8,128)(2,1)S(1)}, u32[]{:S(2)}) copy-start(bf16[16,64,128]{2,1,0:T(8,128)(2,1)S(1)} %collective-permute-done.22.basis_peer) | copy-start | bytes 786436
  206.6 7.8 %copy-start.7 = (bf16[3,8,2,2,64,128]{5,4,3,2,1,0:T(8,128)(2,1)S(1)}, bf16[3,8,2,2,64,128]{5,4,3,2,1,0:T(8,128)(2,1)}, u32[]{:S(2)}) copy-start(bf16[3,8,2,2,64,128]{5,4,3,2,1,0:T(8,128)(2,1)} %constant_dynamic-slice_fusion.16) | copy-start | bytes 4718596
  206.6 9.7 %copy-start.14 = (bf16[4,128,512]{2,1,0:T(8,128)(2,1)S(1)}, bf16[4,128,512]{2,1,0:T(8,128)(2,1)}, u32[]{:S(2)}) copy-start(bf16[4,128,512]{2,1,0:T(8,128)(2,1)} %get-tuple-element.163) | copy-start | bytes 1572868
  206.6 26.4 %collective-permute-start.19 = (bf16[4,128,512]{2,1,0:T(8,128)(2,1)S(1)}, bf16[4,128,512]{2,1,0:T(8,128)(2,1)S(1)}, u32[]{:S(2)}, u32[]{:S(2)}) collective-permute-start(bf16[4,128,512]{2,1,0:T(8,128)(2,1)S(1)} %copy-done.15), channel_id=1, source_target_pairs={{0,28},{1,21},{2,30},{3,23},{4,24},{5,17},{6,26},{7,19},{8,20},{9,... | collective-permute-start | bytes 1572872 | tf_op jit(solution)/shard_map/ppermute | solution.py:300
  214.4 124.9 %collective-permute-start.7 = (bf16[3,8,2,2,64,128]{5,4,3,2,1,0:T(8,128)(2,1)S(1)}, bf16[3,8,2,2,64,128]{5,4,3,2,1,0:T(8,128)(2,1)}, u32[]{:S(2)}, u32[]{:S(2)}) collective-permute-start(bf16[3,8,2,2,64,128]{5,4,3,2,1,0:T(8,128)(2,1)S(1)} %copy-done.7), channel_id=1, source_target_pairs={{0,1},{1,0},{2,3},{3,2},{4,5},{5,4},{6,7},{7,6},{8,9},{9,8},{10,11... | collective-permute-start | bytes 4718600 | tf_op jit(solution)/shard_map/ppermute | solution.py:168
  216.3 23.3 %collective-permute-start.20 = (bf16[4,128,512]{2,1,0:T(8,128)(2,1)S(1)}, bf16[4,128,512]{2,1,0:T(8,128)(2,1)S(1)}, u32[]{:S(2)}, u32[]{:S(2)}) collective-permute-start(bf16[4,128,512]{2,1,0:T(8,128)(2,1)S(1)} %copy-done.14), channel_id=1, source_target_pairs={{0,30},{1,23},{2,28},{3,21},{4,26},{5,19},{6,24},{7,17},{8,22},{9,... | collective-permute-start | bytes 1572872 | tf_op jit(solution)/shard_map/ppermute | solution.py:300
  220.2 30.8 %collective-permute-start.3 = (bf16[4,128,512]{2,1,0:T(8,128)(2,1)}, bf16[4,128,512]{2,1,0:T(8,128)(2,1)S(1)}, u32[]{:S(2)}, u32[]{:S(2)}) collective-permute-start(bf16[4,128,512]{2,1,0:T(8,128)(2,1)} %get-tuple-element.170), channel_id=1, source_target_pairs={{0,0},{1,9},{2,2},{3,11},{4,4},{5,13},{6,6},{7,15},{8,8},{9,1},{10... | collective-permute-start | bytes 1572872 | tf_op jit(solution)/shard_map/ppermute | solution.py:300
  232.9 66.2 %collective-permute-start.4 = (bf16[4,128,512]{2,1,0:T(8,128)(2,1)}, bf16[4,128,512]{2,1,0:T(8,128)(2,1)}, u32[]{:S(2)}, u32[]{:S(2)}) collective-permute-start(bf16[4,128,512]{2,1,0:T(8,128)(2,1)} %get-tuple-element.169), channel_id=1, source_target_pairs={{0,2},{1,11},{2,0},{3,9},{4,6},{5,15},{6,4},{7,13},{8,10},{9,3},{1... | collective-permute-start | bytes 1572872 | tf_op jit(solution)/shard_map/ppermute | solution.py:300
  239.6 68.9 %collective-permute-start.5 = (bf16[4,128,512]{2,1,0:T(8,128)(2,1)}, bf16[4,128,512]{2,1,0:T(8,128)(2,1)}, u32[]{:S(2)}, u32[]{:S(2)}) collective-permute-start(bf16[4,128,512]{2,1,0:T(8,128)(2,1)} %get-tuple-element.168), channel_id=1, source_target_pairs={{0,4},{1,13},{2,6},{3,15},{4,0},{5,9},{6,2},{7,11},{8,12},{9,5},{1... | collective-permute-start | bytes 1572872 | tf_op jit(solution)/shard_map/ppermute | solution.py:300
  240.7 1.9 copy-start.2
  240.8 1.9 copy-start.6
  240.8 81.8 %collective-permute-start.6 = (bf16[4,128,512]{2,1,0:T(8,128)(2,1)}, bf16[4,128,512]{2,1,0:T(8,128)(2,1)S(1)}, u32[]{:S(2)}, u32[]{:S(2)}) collective-permute-start(bf16[4,128,512]{2,1,0:T(8,128)(2,1)} %get-tuple-element.167), channel_id=1, source_target_pairs={{0,6},{1,15},{2,4},{3,13},{4,2},{5,11},{6,0},{7,9},{8,14},{9,7},{1... | collective-permute-start | bytes 1572872 | tf_op jit(solution)/shard_map/ppermute | solution.py:300
  242.6 55.6 %copy-start.10 = (f32[128,256]{1,0:T(8,128)S(1)}, f32[128,256]{1,0:T(8,128)}, u32[]{:S(2)}) copy-start(f32[128,256]{1,0:T(8,128)} %fusion.19) | copy-start | bytes 393220
  242.6 56.5 %copy-start.11 = (bf16[16,2,64,128]{3,2,1,0:T(8,128)(2,1)S(1)}, bf16[16,2,64,128]{3,2,1,0:T(8,128)(2,1)}, u32[]{:S(2)}) copy-start(bf16[16,2,64,128]{3,2,1,0:T(8,128)(2,1)} %constant_dynamic-slice_fusion.14) | copy-start | bytes 1572868
  250.9 57.5 %copy-start.19 = (bf16[16,64,128]{2,1,0:T(8,128)(2,1)S(1)}, bf16[16,64,128]{2,1,0:T(8,128)(2,1)}, u32[]{:S(2)}) copy-start(bf16[16,64,128]{2,1,0:T(8,128)(2,1)} %constant_dynamic-slice_fusion.15) | copy-start | bytes 786436
  250.9 0.8 copy-start.12
  251.8 56.6 %copy-start.13 = (bf16[4,128,512]{2,1,0:T(8,128)(2,1)S(1)}, bf16[4,128,512]{2,1,0:T(8,128)(2,1)}, u32[]{:S(2)}) copy-start(bf16[4,128,512]{2,1,0:T(8,128)(2,1)} %copy-done.12) | copy-start | bytes 1572868
  251.8 100.8 %collective-permute-start.24 = (bf16[2048,256]{1,0:T(8,128)(2,1)}, bf16[2048,256]{1,0:T(8,128)(2,1)S(1)}, u32[]{:S(2)}, u32[]{:S(2)}) collective-permute-start(bf16[2048,256]{1,0:T(8,128)(2,1)} %get-tuple-element.121), channel_id=1, source_target_pairs={{0,1},{1,0},{2,3},{3,2},{4,5},{5,4},{6,7},{7,6},{8,9},{9,8},{10,11... | collective-permute-start | bytes 3145736 | tf_op jit(solution)/shard_map/ppermute | solution.py:168
  299.2 40.0 %collective-permute-start.9 = (bf16[16,2,64,128]{3,2,1,0:T(8,128)(2,1)S(1)}, bf16[16,2,64,128]{3,2,1,0:T(8,128)(2,1)S(1)}, u32[]{:S(2)}, u32[]{:S(2)}) collective-permute-start(bf16[16,2,64,128]{3,2,1,0:T(8,128)(2,1)S(1)} %copy-done.11), channel_id=1, source_target_pairs={{0,1},{1,0},{2,3},{3,2},{4,5},{5,4},{6,7},{7,6},{8,9},{9,8},{10,11... | collective-permute-start | bytes 1572872 | tf_op jit(solution)/shard_map/ppermute | solution.py:168
  308.5 30.7 %collective-permute-start.8 = (bf16[16,64,128]{2,1,0:T(8,128)(2,1)S(1)}, bf16[16,64,128]{2,1,0:T(8,128)(2,1)S(1)}, u32[]{:S(2)}, u32[]{:S(2)}) collective-permute-start(bf16[16,64,128]{2,1,0:T(8,128)(2,1)S(1)} %copy-done.19), channel_id=1, source_target_pairs={{0,1},{1,0},{2,3},{3,2},{4,5},{5,4},{6,7},{7,6},{8,9},{9,8},{10,11... | collective-permute-start | bytes 786440 | tf_op jit(solution)/shard_map/ppermute | solution.py:168
  322.7 16.6 %copy-start.3 = (bf16[16,128,512]{2,1,0:T(8,128)(2,1)}, bf16[16,128,512]{2,1,0:T(8,128)(2,1)S(1)}, u32[]{:S(2)}) copy-start(bf16[16,128,512]{2,1,0:T(8,128)(2,1)S(1)} %constant_dynamic-update-slice_fusion.23.mixed) | copy-start | bytes 6291460
  339.2 0.7 copy-start.18
  339.2 0.9 copy-start.16
  349.5 23.3 %collective-permute-start.26 = (bf16[1792,256]{1,0:T(8,128)(2,1)S(1)}, bf16[1792,256]{1,0:T(8,128)(2,1)S(1)}, u32[]{:S(2)}, u32[]{:S(2)}) collective-permute-start(bf16[1792,256]{1,0:T(8,128)(2,1)S(1)} %slice.142), channel_id=1, source_target_pairs={{0,1},{1,0},{2,3},{3,2},{4,5},{5,4},{6,7},{7,6},{8,9},{9,8},{10,11... | collective-permute-start | bytes 2752520 | tf_op jit(solution)/shard_map/ppermute | solution.py:168
  352.3 22.4 %collective-permute-start.27 = (bf16[256,256]{1,0:T(8,128)(2,1)S(1)}, bf16[256,256]{1,0:T(8,128)(2,1)S(1)}, u32[]{:S(2)}, u32[]{:S(2)}) collective-permute-start(bf16[256,256]{1,0:T(8,128)(2,1)S(1)} %slice.144), channel_id=1, source_target_pairs={{0,1},{1,0},{2,3},{3,2},{4,5},{5,4},{6,7},{7,6},{8,9},{9,8},{10,11... | collective-permute-start | bytes 393224 | tf_op jit(solution)/shard_map/ppermute | solution.py:168

commit v2 on v1

--- a/solution.py
+++ b/solution.py
@@ -173,19 +173,36 @@
     edge_pairs = [(i, j) for i in range(REACH) for j in range(REACH - i)]
     reach_rows = REACH * rows
 
+    def row_sums(near, at, left):
+        blocks = lax.dynamic_slice_in_dim(near, at, REACH, 0).astype(jnp.float32)
+        offset = lax.dynamic_slice_in_dim(near_offsets, at, REACH, 0)
+        blocks = jnp.where(left, blocks[::-1], blocks)
+        offset = jnp.where(left, -offset[::-1], offset)
+        sums = []
+        for row, source in edge_pairs:
+            reads = (offset[row] == -(row + source + 1))[:, None, None]
+            sums.append(jnp.sum(jnp.where(reads, blocks[row], 0.0), axis=0).astype(near.dtype))
+        return sums
+
     def edge_sums(near, mine_too):
         sums = []
         for i, own in zip(edges, owns):
             left = own if mine_too else ~own
-            at = (i + 1) * chunk - jnp.where(left, REACH, 0)
-            blocks = lax.dynamic_slice_in_dim(near, at, REACH, 0).astype(jnp.float32)
-            offset = lax.dynamic_slice_in_dim(near_offsets, at, REACH, 0)
-            blocks = jnp.where(left, blocks[::-1], blocks)
-            offset = jnp.where(left, -offset[::-1], offset)
-            for row, source in edge_pairs:
-                reads = (offset[row] == -(row + source + 1))[:, None, None]
-                sums.append(jnp.sum(jnp.where(reads, blocks[row], 0.0), axis=0).astype(near.dtype))
+            sums += row_sums(near, (i + 1) * chunk - jnp.where(left, REACH, 0), left)
         return jnp.stack(sums)
+
+    def side(device):
+        return parity(device >> bits)
+
+    def moved(other):
+        other_parity = sum((((other >> bits) >> k) & 1) for k in range(chunks.bit_length())) & 1
+        return (other >= 0) & (other < leafs) & (other_parity != home_parity)
+
+    assert span > 1
+    low_moved, high_moved = moved(d - 1), moved(d + 1)
+    ends = [(a, a + 1) for a in range(leafs - 1) if side(a) != side(a + 1)]
+    end_pairs = [(2 * a + side(a), 2 * a + 1 - side(a)) for pair in ends for a in pair]
+    end_rows = jnp.where(high_moved, box_count - REACH, 0)
 
     half_pairs = chunk // 2
     pool = {
@@ -200,7 +217,7 @@
     queue = [(name, s) for s in range(steps) for name in ("source", "rhs", "source_blocks")]
     for s in range(steps):
         queue += [(name, s) for name in ("target_blocks", "target", "near")]
-    queue += ["edges"]
+    queue += ["edges", "ends"]
     first_cut = pl.pallas_call(
         functools.partial(cut_kernel, span=span, masks=[masks[0][0], masks[1][0]]),
         out_shape=pltpu.VMEM((chunk, half, rows), rhs.dtype),
@@ -209,15 +226,18 @@
         scratch_shapes=[pltpu.SemaphoreType.DMA],
         name="first_cut",
     )
+    both = ("leaf", "rhs")
     received = {}
     for n, entry in enumerate(queue):
         if entry == "edges":
             piece = edge_sums(arrays["near"], True)
+        elif entry == "ends":
+            piece = jnp.stack(row_sums(arrays["near"], end_rows, high_moved))
         else:
             name, s = entry
             piece = cut(arrays[name], others[s], pool[name][1], pool[name][2]) if n else first_cut(arrays[name])
         piece, arrays = lax.optimization_barrier((piece, arrays))
-        received[entry] = swap(piece)
+        received[entry] = lax.ppermute(piece, both, end_pairs) if entry == "ends" else swap(piece)
 
     peer_rhs = jnp.zeros(((box_count + 2 * REACH) * rows, columns), rhs.dtype)
     for s in range(steps):
@@ -228,29 +248,16 @@
     peer_head = peer_rhs[reach_rows : 2 * reach_rows]
     up = [(i, i + 1) for i in range(leafs - 1)]
     down = [(i + 1, i) for i in range(leafs - 1)]
-    tail = rhs[-reach_rows:]
-    head = rhs[:reach_rows]
-
-    def side(device):
-        return parity(device >> bits)
-
-    def same_side(other):
-        return (sum((((other >> bits) >> k) & 1) for k in range(chunks.bit_length())) & 1) == home_parity
-
-    both = ("leaf", "rhs")
-    low_peer = lax.ppermute(
-        jnp.where(same_side(d + 1), peer_tail, tail), both,
-        [(2 * a + side(a), 2 * b + side(b)) for a, b in up],
-    )
-    high_peer = lax.ppermute(
-        jnp.where(same_side(d - 1), peer_head, head), both,
-        [(2 * a + side(a), 2 * b + side(b)) for a, b in down],
-    )
+    ends_in = []
+    for rows_out, way in ((arrays["rhs"][-reach_rows:], up), (arrays["rhs"][:reach_rows], down)):
+        ends_in.append(lax.ppermute(rows_out, "leaf", way))
+    for rows_out, way in ((peer_tail, up), (peer_head, down)):
+        pairs = [(2 * a + side(a), 2 * b + side(b)) for a, b in way if side(a) == side(b)]
+        ends_in.append(lax.ppermute(rows_out, both, pairs))
+    low_own, high_own, low_peer, high_peer = ends_in
     peer_rhs = lax.dynamic_update_slice_in_dim(peer_rhs, low_peer, 0, 0)
     peer_rhs = lax.dynamic_update_slice_in_dim(peer_rhs, high_peer, box_count * rows + reach_rows, 0)
-    own_rhs = jnp.concatenate(
-        [lax.ppermute(tail, "leaf", up), rhs, lax.ppermute(head, "leaf", down)], axis=0
-    )
+    own_rhs = jnp.concatenate([low_own, rhs, high_own], axis=0)
 
     params = pltpu.CompilerParams(
         dimension_semantics=("arbitrary",), vmem_limit_bytes=56 * 2**20
@@ -344,42 +351,58 @@
         )
         product, send = far(*operands)
         at = others[s] * (chunk * rows)
-        most = chunk * rows if s < steps - 1 else chunk * rows * 7 // 8
-        for a, b in ((0, most), (most, chunk * rows)):
-            if a < b:
-                returned.append((swap(send[a:b]), at, a, b))
-
-    own_sums, peer_sums = edge_sums(near_t, False), received["edges"]
-    sums = jnp.where(
-        h == 0,
-        jnp.concatenate([own_sums, peer_sums], axis=1),
-        jnp.concatenate([peer_sums, own_sums], axis=1),
-    )
-    at_edges = []
-    for n, (i, own) in enumerate(zip(edges, owns)):
-        sources = lax.dynamic_slice_in_dim(rhs, ((i + 1) * chunk - jnp.where(own, REACH, 0)) * rows, reach_rows, 0)
+        size = chunk * rows
+        spans = [(0, size)]
+        if s == steps - 1:
+            middle = size // 2
+            spans = [(0, middle - rows), (middle + rows, size), (middle - rows, middle + rows)]
+        for a, b in spans:
+            returned.append((s, swap(send[a:b]), at, a, b))
+
+    own_sums = [edge_sums(near_t, False), jnp.stack(row_sums(near_t, end_rows, high_moved))]
+
+    def products_of(own, peer, sources, left):
+        sums = jnp.where(
+            h == 0, jnp.concatenate([own, peer], axis=1), jnp.concatenate([peer, own], axis=1)
+        )
         sources = sources.reshape(REACH, rows, columns)
-        sources = jnp.where(own, sources[::-1], sources)
+        sources = jnp.where(left, sources[::-1], sources)
         products = [jnp.zeros((rows, columns), jnp.float32) for _ in range(REACH)]
         for p, (row, source) in enumerate(edge_pairs):
             products[row] += lax.dot_general(
-                sums[n * len(edge_pairs) + p], sources[source], (((0,), (0,)), ((), ())),
-                preferred_element_type=jnp.float32,
+                sums[p], sources[source], (((0,), (0,)), ((), ())), preferred_element_type=jnp.float32
             )
         products = jnp.stack(products)
-        at_edges.append(jnp.where(own, products, products[::-1]).reshape(reach_rows, columns))
+        return jnp.where(left, products, products[::-1]).reshape(reach_rows, columns)
+
+    count = len(edge_pairs)
+    at_edges = []
+    for n, (i, own) in enumerate(zip(edges, owns)):
+        start = (i + 1) * chunk - jnp.where(own, REACH, 0)
+        at_edges.append(
+            products_of(
+                own_sums[0][n * count : (n + 1) * count],
+                received["edges"][n * count : (n + 1) * count],
+                lax.dynamic_slice_in_dim(arrays["rhs"], start * rows, reach_rows, 0),
+                own,
+            )
+        )
     at_edges = jnp.concatenate(at_edges, axis=0)
+    at_end = products_of(
+        own_sums[1], received["ends"], jnp.where(high_moved, high_own, low_own), ~high_moved
+    )
+    at_end = jnp.where((low_moved | high_moved) & (home_parity != h), at_end, 0.0)
     added = []
     for s in range(steps):
-        products = cut(at_edges, others[s] >> 1, reach_rows)
-        place = jnp.where(others[s] & 1, 0, (chunk - REACH) * rows)
-        added.append(
-            lax.dynamic_update_slice_in_dim(
-                jnp.zeros((chunk * rows, columns), jnp.float32), products, place, 0
-            )
-        )
-    for s, (part, at, a, b) in zip([*range(steps), steps - 1], returned):
-        part = (part.astype(jnp.float32) + added[s][a:b]).astype(rhs.dtype)
+        inner = cut(at_edges, others[s] >> 1, reach_rows)
+        first = jnp.where(others[s] & 1, inner, jnp.where((others[s] == 0) & ~high_moved, at_end, 0.0))
+        last = jnp.where(others[s] & 1, jnp.where((others[s] == chunks - 1) & high_moved, at_end, 0.0), inner)
+        middle = jnp.zeros(((chunk - 2 * REACH) * rows, columns), jnp.float32)
+        added.append(jnp.concatenate([first, middle, last], axis=0))
+    added = lax.optimization_barrier(added)
+    for s, part, at, a, b in returned:
+        if a < reach_rows or b > chunk * rows - reach_rows:
+            part = (part.astype(jnp.float32) + added[s][a:b]).astype(rhs.dtype)
         product = lax.dynamic_update_slice_in_dim(product, part, at + a, 0)
     return product
 

time: 376 us -> 349 us (0.928)
  waiting for transfers between devices: 172 us -> 154 us
  local copies, waits for them, and re-layouts: 53 us -> 46.8 us
    ppermute x16 -> x17, starting transfers between devices: 83.9 us -> 69.4 us  [swap(): return lax.ppermute(array, 'rhs', SWAP)]
    ppermute x8, starting transfers between devices: 13.1 us -> 25.8 us  [on_device(): piece = lax.ppermute(cut(mixed, slot, quota), both, pairs)]
    ppermute x8, waiting for transfers between devices: 15.9 us -> 3.33 us  [on_device(): piece = lax.ppermute(cut(mixed, slot, quota), both, pairs)]
    unnamed x55 -> x51, local copies, waits for them, and re-layouts: 8.88 us -> 1.19 us
    ppermute x16 -> x17, waiting for transfers between devices: 157 us -> 151 us  [swap(): return lax.ppermute(array, 'rhs', SWAP)]
    ppermute x4 -> x5, starting transfers between devices: 8.47 us -> 7.71 us  [the longest x2 4.47 us: on_device(): ends_in.append(lax.ppermute(rows_out, both, pairs))]
  transfers between devices with their start and end apart: 28 -> 30, of which waited for: 9 -> 10; matrix products, arithmetic and copies ran while one was open for 10% -> 14% of each run, Pallas kernels for 8% -> 9%
where the time goes in v2:
time: 349 us; the launch traced here: 348 us
  waiting for transfers between devices  154 us (44%)
  starting transfers between devices  103 us (30%)
  local copies, waits for them, and re-layouts  46.8 us (13%)
  Pallas kernels  30.9 us (9%)
  other arithmetic  10.4 us (3%)
    ppermute x17, waiting for transfers between devices, swap(): return lax.ppermute(array, 'rhs', SWAP)  151 us
    ppermute x17, starting transfers between devices, swap(): return lax.ppermute(array, 'rhs', SWAP)  69.4 us
    dynamic_slice x13, local copies, waits for them, and re-layouts, cut(): return lax.dynamic_slice_in_dim(array, at * size, size, axis)  26.6 us
    ppermute x8, starting transfers between devices, on_device(): piece = lax.ppermute(cut(mixed, slot, quota), both, pairs)  25.8 us
    pallas_call x2, Pallas kernels, on_device(): product, send = far(*operands)  16.4 us
    pallas_call x2, Pallas kernels, on_device(): pl.pallas_call(source_kernel, out_shape=jax.ShapeDtypeStruct((chunk, rank...  13.6 us
    dynamic_update_slice x8, local copies, waits for them, and re-layouts, on_device(): arrived = lax.dynamic_update_slice_in_dim(arrived, piece, slot * quota, 0)  7.61 us
  transfers between devices with their start and end apart: 30, of which 10 were waited for; matrix products, arithmetic and copies ran while one was open for 14% of the time, Pallas kernels for 9%

profile of v2, /device:TPU:0, one launch (start us, length us, event | category | flops | bytes accessed | tf_op | source)
XLA Modules:
  0.0 347.9 jit_solution(3195555176526077408)
XLA Ops:
  0.0 1.0 first_cut.1
  1.0 2.3 constant_dynamic-slice_fusion.29
  3.3 2.8 constant_dynamic-slice_fusion.28
  6.0 1.7 constant_dynamic-slice_fusion.27
  7.7 2.3 constant_dynamic-slice_fusion.26
  10.0 3.0 collective-permute-start
  13.0 2.8 constant_dynamic-slice_fusion.25
  15.8 2.0 collective-permute-start.2
  17.8 2.8 constant_dynamic-slice_fusion.20
  21.3 0.9 constant_dynamic-slice_fusion.18
  22.2 2.8 constant_dynamic-slice_fusion.17
  25.7 0.9 constant_dynamic-slice_fusion.15
  28.1 1.1 constant_dynamic-slice_fusion.2
  29.2 1.3 collective-permute-start.11
  34.3 43.5 %collective-permute-done.25 = bf16[6,64,128]{2,1,0:T(8,128)(2,1)S(1)} collective-permute-done((bf16[6,64,128]{2,1,0:T(8,128)(2,1)S(1)}, bf16[6,64,128]{2,1,0:T(8,128)(2,1)S(1)}, u32[]{:S(2)}, u32[]{:S(2)}) %collective-permute-start.25) | collective-permute-done | bytes 98336 | tf_op jit(solution)/shard_map/ppermute | solution.py:168
  77.8 1.3 collective-permute-start.10
  81.2 1.7 collective-permute-start.12
  84.2 1.8 constant_dynamic-slice_fusion.5
  86.0 20.7 %collective-permute-done.12.rhs_peer = bf16[2048,256]{1,0:T(8,128)(2,1)S(1)} collective-permute-done((bf16[2048,256]{1,0:T(8,128)(2,1)}, bf16[2048,256]{1,0:T(8,128)(2,1)S(1)}, u32[]{:S(2)}, u32[]{:S(2)}) %collective-permute-start.12) | collective-permute-done | bytes 1048608 | tf_op jit(solution)/shard_map/ppermute | solution.py:168
  106.7 1.7 collective-permute-start.15
  108.9 1.3 constant_dynamic-update-slice_fusion.16
  110.2 3.2 collective-permute-start.13
  113.4 1.0 broadcast_select_fusion.1
  115.1 31.0 %collective-permute-done.15.basis_peer = bf16[16,64,128]{2,1,0:T(8,128)(2,1)} collective-permute-done((bf16[16,64,128]{2,1,0:T(8,128)(2,1)S(1)}, bf16[16,64,128]{2,1,0:T(8,128)(2,1)}, u32[]{:S(2)}, u32[]{:S(2)}) %collective-permute-start.15) | collective-permute-done | bytes 262176 | tf_op jit(solution)/shard_map/ppermute | solution.py:168
  146.1 1.7 collective-permute-start.21
  147.9 1.3 collective-permute-start.14
  149.2 6.8 %shard_map.92 = bf16[16,128,512]{2,1,0:T(8,128)(2,1)} custom-call(s32[2]{0:T(128)} %pad_add_fusion.1.idx, bf16[8192,256]{1,0:T(8,128)(2,1)} %rhs_own.3, bf16[2048,256]{1,0:T(8,128)(2,1)} %copy-done.5, bf16[64,64,128]{2,1,0:T(8,128)(2,1)} %bitcast.213, bf16[16,64,128]{2,1,0:T(8,128)(2,1)} %collective-permute-done.15.basis_peer, ...), custom_call_target="tpu_custom_call" | custom-call | tf_op jit(solution)/shard_map/pallas_call | solution.py:289
  156.0 3.0 constant_dynamic-slice_fusion.6
  159.0 9.0 %collective-permute-start.17 = (bf16[4,128,512]{2,1,0:T(8,128)(2,1)}, bf16[4,128,512]{2,1,0:T(8,128)(2,1)}, u32[]{:S(2)}, u32[]{:S(2)}) collective-permute-start(bf16[4,128,512]{2,1,0:T(8,128)(2,1)} %get-tuple-element.205), channel_id=1, source_target_pairs={{0,24},{1,17},{2,26},{3,19},{4,28},{5,21},{6,30},{7,23},{8,16},{9,... | collective-permute-start | bytes 1572872 | tf_op jit(solution)/shard_map/ppermute | solution.py:307
  168.0 0.8 collective-permute-start.18
  169.1 3.8 %collective-permute-start.20 = (bf16[4,128,512]{2,1,0:T(8,128)(2,1)}, bf16[4,128,512]{2,1,0:T(8,128)(2,1)}, u32[]{:S(2)}, u32[]{:S(2)}) collective-permute-start(bf16[4,128,512]{2,1,0:T(8,128)(2,1)} %get-tuple-element.202), channel_id=1, source_target_pairs={{0,30},{1,23},{2,28},{3,21},{4,26},{5,19},{6,24},{7,17},{8,22},{9,... | collective-permute-start | bytes 1572872 | tf_op jit(solution)/shard_map/ppermute | solution.py:307
  173.0 1.1 bitcast_select_fusion.1
  174.1 6.8 %shard_map.91 = bf16[16,128,512]{2,1,0:T(8,128)(2,1)} custom-call(s32[2]{0:T(128)} %pad_add_fusion.idx, bf16[8192,256]{1,0:T(8,128)(2,1)} %rhs_own.3, bf16[2048,256]{1,0:T(8,128)(2,1)} %collective-permute-done.rhs_peer, bf16[64,64,128]{2,1,0:T(8,128)(2,1)} %bitcast.214, bf16[16,64,128]{2,1,0:T(8,128)(2,1)} %collective-permute-done.1.basis_peer, ...), custom_call_target="tpu_custom_call" | custom-call | tf_op jit(solution)/shard_map/pallas_call | solution.py:289
  180.9 3.1 constant_dynamic-slice_fusion.21
  184.0 39.5 %collective-permute-start.7 = (bf16[3,8,2,2,64,128]{5,4,3,2,1,0:T(8,128)(2,1)S(1)}, bf16[3,8,2,2,64,128]{5,4,3,2,1,0:T(8,128)(2,1)}, u32[]{:S(2)}, u32[]{:S(2)}) collective-permute-start(bf16[3,8,2,2,64,128]{5,4,3,2,1,0:T(8,128)(2,1)S(1)} %copy-done.8), channel_id=1, source_target_pairs={{0,1},{1,0},{2,3},{3,2},{4,5},{5,4},{6,7},{7,6},{8,9},{9,8},{10,11... | collective-permute-start | bytes 4718600 | tf_op jit(solution)/shard_map/ppermute | solution.py:168
  223.6 7.7 %collective-permute-start.23 = (bf16[16,2,64,128]{3,2,1,0:T(8,128)(2,1)S(1)}, bf16[16,2,64,128]{3,2,1,0:T(8,128)(2,1)S(1)}, u32[]{:S(2)}, u32[]{:S(2)}) collective-permute-start(bf16[16,2,64,128]{3,2,1,0:T(8,128)(2,1)S(1)} %copy-done.18), channel_id=1, source_target_pairs={{0,1},{1,0},{2,3},{3,2},{4,5},{5,4},{6,7},{7,6},{8,9},{9,8},{10,11... | collective-permute-start | bytes 1572872 | tf_op jit(solution)/shard_map/ppermute | solution.py:168
  231.3 5.3 %collective-permute-start.3 = (bf16[4,128,512]{2,1,0:T(8,128)(2,1)}, bf16[4,128,512]{2,1,0:T(8,128)(2,1)}, u32[]{:S(2)}, u32[]{:S(2)}) collective-permute-start(bf16[4,128,512]{2,1,0:T(8,128)(2,1)} %get-tuple-element.211), channel_id=1, source_target_pairs={{0,0},{1,9},{2,2},{3,11},{4,4},{5,13},{6,6},{7,15},{8,8},{9,1},{10... | collective-permute-start | bytes 1572872 | tf_op jit(solution)/shard_map/ppermute | solution.py:307
  236.6 3.4 collective-permute-start.4
  240.0 1.7 constant_dynamic-slice_fusion.4
  241.8 1.1 constant_dynamic-update-slice_fusion.13
  242.9 1.1 constant_dynamic-update-slice_fusion.12
  244.0 1.1 constant_dynamic-update-slice_fusion.11
  245.1 1.1 constant_dynamic-update-slice_fusion.10.mixed
  246.2 20.9 %collective-permute-done.23.near_peer = bf16[16,2,64,128]{3,2,1,0:T(8,128)(2,1)S(1)} collective-permute-done((bf16[16,2,64,128]{3,2,1,0:T(8,128)(2,1)S(1)}, bf16[16,2,64,128]{3,2,1,0:T(8,128)(2,1)S(1)}, u32[]{:S(2)}, u32[]{:S(2)}) %collective-permute-start.23) | collective-permute-done | bytes 524320 | tf_op jit(solution)/shard_map/ppermute | solution.py:168
  267.1 1.9 collective-permute-start.9
  269.0 2.1 collective-permute-start.5
  271.2 8.2 %shard_map.93 = (bf16[8192,256]{1,0:T(8,128)(2,1)}, bf16[2048,256]{1,0:T(8,128)(2,1)}) custom-call(s32[2]{0:T(128)} %pad_add_fusion.1.idx, s32[128]{0:T(128)} %reshape.283.offsets, bf16[16,128,512]{2,1,0:T(8,128)(2,1)} %copy-done.2, bf16[3,32,2,2,64,128]{5,4,3,2,1,0:T(8,128)(2,1)} %own.7, bf16[3,8,2,2,64,128]{5,4,3,2,1,0:T(8,128)(2,1)} %copy-done.6, ...), custom_call_target="tpu_custom_call" | custom-call | tf_op jit(solution)/shard_map/pallas_call | solution.py:352
  279.5 1.0 collective-permute-start.6
  281.5 1.1 constant_dynamic-update-slice_fusion.21
  282.6 1.6 collective-permute-done.5
  284.3 6.3 %collective-permute-start.8 = (bf16[16,64,128]{2,1,0:T(8,128)(2,1)S(1)}, bf16[16,64,128]{2,1,0:T(8,128)(2,1)S(1)}, u32[]{:S(2)}, u32[]{:S(2)}) collective-permute-start(bf16[16,64,128]{2,1,0:T(8,128)(2,1)S(1)} %copy-done.20), channel_id=1, source_target_pairs={{0,1},{1,0},{2,3},{3,2},{4,5},{5,4},{6,7},{7,6},{8,9},{9,8},{10,11... | collective-permute-start | bytes 786440 | tf_op jit(solution)/shard_map/ppermute | solution.py:168
  290.6 1.1 constant_dynamic-update-slice_fusion.20
  291.6 1.1 constant_dynamic-update-slice_fusion.19
  292.7 1.7 collective-permute-done.6
  294.5 17.2 %collective-permute-done.8.basis_peer = bf16[16,64,128]{2,1,0:T(8,128)(2,1)S(1)} collective-permute-done((bf16[16,64,128]{2,1,0:T(8,128)(2,1)S(1)}, bf16[16,64,128]{2,1,0:T(8,128)(2,1)S(1)}, u32[]{:S(2)}, u32[]{:S(2)}) %collective-permute-start.8) | collective-permute-done | bytes 262176 | tf_op jit(solution)/shard_map/ppermute | solution.py:168
  312.4 8.1 %shard_map.94 = (bf16[8192,256]{1,0:T(8,128)(2,1)}, bf16[2048,256]{1,0:T(8,128)(2,1)}) custom-call(s32[2]{0:T(128)} %pad_add_fusion.idx, s32[128]{0:T(128)} %reshape.283.offsets, bf16[16,128,512]{2,1,0:T(8,128)(2,1)} %copy-done.3, bf16[3,32,2,2,64,128]{5,4,3,2,1,0:T(8,128)(2,1)} %own.7, ...), custom_call_target="tpu_custom_call", output_to_operand_aliasing={{0}: (12, {})} | custom-call | tf_op jit(solution)/shard_map/pallas_call | solution.py:352
  320.5 0.9 slice.212
  321.4 1.2 fusion.25
  323.3 1.4 collective-permute-start.28
  325.3 2.4 fusion.3
  327.8 8.3 %collective-permute-done.27 = bf16[896,256]{1,0:T(8,128)(2,1)S(1)} collective-permute-done((bf16[896,256]{1,0:T(8,128)(2,1)S(1)}, bf16[896,256]{1,0:T(8,128)(2,1)S(1)}, u32[]{:S(2)}, u32[]{:S(2)}) %collective-permute-start.27) | collective-permute-done | bytes 458784 | tf_op jit(solution)/shard_map/ppermute | solution.py:168
  336.1 0.9 fusion.4
  337.0 8.8 %collective-permute-done.28 = bf16[896,256]{1,0:T(8,128)(2,1)S(1)} collective-permute-done((bf16[896,256]{1,0:T(8,128)(2,1)S(1)}, bf16[896,256]{1,0:T(8,128)(2,1)S(1)}, u32[]{:S(2)}, u32[]{:S(2)}) %collective-permute-start.28) | collective-permute-done | bytes 458784 | tf_op jit(solution)/shard_map/ppermute | solution.py:168
  345.8 0.9 fusion.5
  (151 shorter events, 15.8 us)
Async XLA Ops:
  10.0 98.9 %collective-permute-start = (bf16[2048,256]{1,0:T(8,128)(2,1)}, bf16[2048,256]{1,0:T(8,128)(2,1)}, u32[]{:S(2)}, u32[]{:S(2)}) collective-permute-start(bf16[2048,256]{1,0:T(8,128)(2,1)} %constant_dynamic-slice_fusion.26), channel_id=1, source_target_pairs={{0,1},{1,0},{2,3},{3,2},{4,5},{5,4},{6,7},{7,6},{8,9},{9,8},{10,11... | collective-permute-start | bytes 3145736 | tf_op jit(solution)/shard_map/ppermute | solution.py:168
  13.0 146.0 %collective-permute-start.1 = (bf16[16,64,128]{2,1,0:T(8,128)(2,1)}, bf16[16,64,128]{2,1,0:T(8,128)(2,1)}, u32[]{:S(2)}, u32[]{:S(2)}) collective-permute-start(bf16[16,64,128]{2,1,0:T(8,128)(2,1)} %constant_dynamic-slice_fusion.27), channel_id=1, source_target_pairs={{0,1},{1,0},{2,3},{3,2},{4,5},{5,4},{6,7},{7,6},{8,9},{9,8},{10,11... | collective-permute-start | bytes 786440 | tf_op jit(solution)/shard_map/ppermute | solution.py:168
  15.8 4.8 %copy-start.4 = (bf16[64,128,64]{1,2,0:T(8,128)(2,1)S(1)}, bf16[64,128,64]{1,2,0:T(8,128)(2,1)}, u32[]{:S(2)}) copy-start(bf16[64,128,64]{1,2,0:T(8,128)(2,1)} %param.11) | copy-start | bytes 3145732
  15.8 5.5 %copy-start.1 = (bf16[64,2,128,64]{2,3,1,0:T(8,128)(2,1)S(1)}, bf16[64,2,128,64]{2,3,1,0:T(8,128)(2,1)}, u32[]{:S(2)}) copy-start(bf16[64,2,128,64]{2,3,1,0:T(8,128)(2,1)} %param.12) | copy-start | bytes 6291460
  15.8 153.3 %collective-permute-start.2 = (bf16[3,8,2,2,64,128]{5,4,3,2,1,0:T(8,128)(2,1)}, bf16[3,8,2,2,64,128]{5,4,3,2,1,0:T(8,128)(2,1)}, u32[]{:S(2)}, u32[]{:S(2)}) collective-permute-start(bf16[3,8,2,2,64,128]{5,4,3,2,1,0:T(8,128)(2,1)} %constant_dynamic-slice_fusion.25), channel_id=1, source_target_pairs={{0,1},{1,0},{2,3},{3,2},{4,5},{5,4},{6,7},{7,6},{8,9},{9,8},{10,11... | collective-permute-start | bytes 4718600 | tf_op jit(solution)/shard_map/ppermute | solution.py:168
  24.9 1.7 copy-start.21
  29.2 51.9 %collective-permute-start.11 = (bf16[256,256]{1,0:T(8,128)(2,1)S(1)}, bf16[256,256]{1,0:T(8,128)(2,1)S(1)}, u32[]{:S(2)}, u32[]{:S(2)}) collective-permute-start(bf16[256,256]{1,0:T(8,128)(2,1)S(1)} %get-tuple-element.197), channel_id=1, source_target_pairs={{2,0},{4,2},{6,4},{8,6},{10,8},{12,10},{14,12},{16,14},{18,16},{20... | collective-permute-start | bytes 393224 | tf_op jit(solution)/shard_map/ppermute | solution.py:253
  30.5 3.5 %collective-permute-start.26 = (bf16[3,64,128]{2,1,0:T(8,128)(2,1)S(1)}, bf16[3,64,128]{2,1,0:T(8,128)(2,1)S(1)}, u32[]{:S(2)}, u32[]{:S(2)}) collective-permute-start(bf16[3,64,128]{2,1,0:T(8,128)(2,1)S(1)} %pad_maximum_fusion.5), channel_id=1, source_target_pairs={{6,7},{9,8},{23,22},{24,25}} | collective-permute-start | bytes 147464 | tf_op jit(solution)/shard_map/ppermute | solution.py:240
  34.0 43.7 %collective-permute-start.25 = (bf16[6,64,128]{2,1,0:T(8,128)(2,1)S(1)}, bf16[6,64,128]{2,1,0:T(8,128)(2,1)S(1)}, u32[]{:S(2)}, u32[]{:S(2)}) collective-permute-start(bf16[6,64,128]{2,1,0:T(8,128)(2,1)S(1)} %constant_dynamic-update-slice_fusion), channel_id=1, source_target_pairs={{0,1},{1,0},{2,3},{3,2},{4,5},{5,4},{6,7},{7,6},{8,9},{9,8},{10,11... | collective-permute-start | bytes 294920 | tf_op jit(solution)/shard_map/ppermute | solution.py:168
  77.8 5.2 %collective-permute-start.10 = (bf16[256,256]{1,0:T(8,128)(2,1)S(1)}, bf16[256,256]{1,0:T(8,128)(2,1)S(1)}, u32[]{:S(2)}, u32[]{:S(2)}) collective-permute-start(bf16[256,256]{1,0:T(8,128)(2,1)S(1)} %get-tuple-element.198), channel_id=1, source_target_pairs={{0,2},{2,4},{4,6},{6,8},{8,10},{10,12},{12,14},{14,16},{16,18},{18... | collective-permute-start | bytes 393224 | tf_op jit(solution)/shard_map/ppermute | solution.py:253
  79.1 4.1 %copy-start = (bf16[8192,256]{1,0:T(8,128)(2,1)S(1)}, bf16[8192,256]{1,0:T(8,128)(2,1)}, u32[]{:S(2)}) copy-start(bf16[8192,256]{1,0:T(8,128)(2,1)} %rhs_own.3) | copy-start | bytes 12582916
  81.2 25.5 %collective-permute-start.12 = (bf16[2048,256]{1,0:T(8,128)(2,1)}, bf16[2048,256]{1,0:T(8,128)(2,1)S(1)}, u32[]{:S(2)}, u32[]{:S(2)}) collective-permute-start(bf16[2048,256]{1,0:T(8,128)(2,1)} %constant_dynamic-slice_fusion.29), channel_id=1, source_target_pairs={{0,1},{1,0},{2,3},{3,2},{4,5},{5,4},{6,7},{7,6},{8,9},{9,8},{10,11... | collective-permute-start | bytes 3145736 | tf_op jit(solution)/shard_map/ppermute | solution.py:168
  82.9 64.9 %collective-permute-start.16 = (bf16[3,8,2,2,64,128]{5,4,3,2,1,0:T(8,128)(2,1)}, bf16[3,8,2,2,64,128]{5,4,3,2,1,0:T(8,128)(2,1)S(1)}, u32[]{:S(2)}, u32[]{:S(2)}) collective-permute-start(bf16[3,8,2,2,64,128]{5,4,3,2,1,0:T(8,128)(2,1)} %constant_dynamic-slice_fusion.28), channel_id=1, source_target_pairs={{0,1},{1,0},{2,3},{3,2},{4,5},{5,4},{6,7},{7,6},{8,9},{9,8},{10,11... | collective-permute-start | bytes 4718600 | tf_op jit(solution)/shard_map/ppermute | solution.py:168
  106.7 2.1 copy-start.5
  106.7 39.4 %collective-permute-start.15 = (bf16[16,64,128]{2,1,0:T(8,128)(2,1)S(1)}, bf16[16,64,128]{2,1,0:T(8,128)(2,1)}, u32[]{:S(2)}, u32[]{:S(2)}) collective-permute-start(bf16[16,64,128]{2,1,0:T(8,128)(2,1)S(1)} %first_cut.1), channel_id=1, source_target_pairs={{0,1},{1,0},{2,3},{3,2},{4,5},{5,4},{6,7},{7,6},{8,9},{9,8},{10,11... | collective-permute-start | bytes 786440 | tf_op jit(solution)/shard_map/ppermute | solution.py:168
  110.2 4.2 %collective-permute-start.13 = (bf16[256,256]{1,0:T(8,128)(2,1)S(1)}, bf16[256,256]{1,0:T(8,128)(2,1)S(1)}, u32[]{:S(2)}, u32[]{:S(2)}) collective-permute-start(bf16[256,256]{1,0:T(8,128)(2,1)S(1)} %slice.219), channel_id=1, source_target_pairs={{0,2},{2,4},{4,6},{9,11},{11,13},{13,15},{15,17},{17,19},{19,21},{... | collective-permute-start | bytes 393224 | tf_op jit(solution)/shard_map/ppermute | solution.py:256
  114.4 53.6 %collective-permute-start.22 = (bf16[16,64,128]{2,1,0:T(8,128)(2,1)}, bf16[16,64,128]{2,1,0:T(8,128)(2,1)}, u32[]{:S(2)}, u32[]{:S(2)}) collective-permute-start(bf16[16,64,128]{2,1,0:T(8,128)(2,1)} %constant_dynamic-slice_fusion.19), channel_id=1, source_target_pairs={{0,1},{1,0},{2,3},{3,2},{4,5},{5,4},{6,7},{7,6},{8,9},{9,8},{10,11... | collective-permute-start | bytes 786440 | tf_op jit(solution)/shard_map/ppermute | solution.py:168
  146.1 122.9 %collective-permute-start.21 = (bf16[3,8,2,2,64,128]{5,4,3,2,1,0:T(8,128)(2,1)}, bf16[3,8,2,2,64,128]{5,4,3,2,1,0:T(8,128)(2,1)S(1)}, u32[]{:S(2)}, u32[]{:S(2)}) collective-permute-start(bf16[3,8,2,2,64,128]{5,4,3,2,1,0:T(8,128)(2,1)} %constant_dynamic-slice_fusion.20), channel_id=1, source_target_pairs={{0,1},{1,0},{2,3},{3,2},{4,5},{5,4},{6,7},{7,6},{8,9},{9,8},{10,11... | collective-permute-start | bytes 4718600 | tf_op jit(solution)/shard_map/ppermute | solution.py:168
  147.9 1.3 copy-start.7
  147.9 20.9 %collective-permute-start.14 = (bf16[256,256]{1,0:T(8,128)(2,1)}, bf16[256,256]{1,0:T(8,128)(2,1)S(1)}, u32[]{:S(2)}, u32[]{:S(2)}) collective-permute-start(bf16[256,256]{1,0:T(8,128)(2,1)} %get-tuple-element.193), channel_id=1, source_target_pairs={{2,0},{4,2},{6,4},{11,9},{13,11},{15,13},{17,15},{19,17},{21,19},{... | collective-permute-start | bytes 393224 | tf_op jit(solution)/shard_map/ppermute | solution.py:256
  156.0 17.0 %copy-start.12 = (f32[2,128,256]{2,1,0:T(8,128)S(1)}, f32[2,128,256]{2,1,0:T(8,128)}, u32[]{:S(2)}) copy-start(f32[2,128,256]{2,1,0:T(8,128)} %reverse_select_fusion.2) | copy-start | bytes 786436
  156.0 17.0 %copy-start.13 = (f32[2,128,256]{2,1,0:T(8,128)S(1)}, f32[2,128,256]{2,1,0:T(8,128)}, u32[]{:S(2)}) copy-start(f32[2,128,256]{2,1,0:T(8,128)} %get-tuple-element.218) | copy-start | bytes 786436
  156.0 17.0 %copy-start.14 = (f32[2,128,256]{2,1,0:T(8,128)S(1)}, f32[2,128,256]{2,1,0:T(8,128)}, u32[]{:S(2)}) copy-start(f32[2,128,256]{2,1,0:T(8,128)} %get-tuple-element.219) | copy-start | bytes 786436
  156.0 17.0 %copy-start.15 = (f32[2,128,256]{2,1,0:T(8,128)S(1)}, f32[2,128,256]{2,1,0:T(8,128)}, u32[]{:S(2)}) copy-start(f32[2,128,256]{2,1,0:T(8,128)} %get-tuple-element.220) | copy-start | bytes 786436
  156.0 17.0 %copy-start.16 = (f32[2,128,256]{2,1,0:T(8,128)S(1)}, f32[2,128,256]{2,1,0:T(8,128)}, u32[]{:S(2)}) copy-start(f32[2,128,256]{2,1,0:T(8,128)} %get-tuple-element.221) | copy-start | bytes 786436
  159.0 25.0 %collective-permute-start.17 = (bf16[4,128,512]{2,1,0:T(8,128)(2,1)}, bf16[4,128,512]{2,1,0:T(8,128)(2,1)}, u32[]{:S(2)}, u32[]{:S(2)}) collective-permute-start(bf16[4,128,512]{2,1,0:T(8,128)(2,1)} %get-tuple-element.205), channel_id=1, source_target_pairs={{0,24},{1,17},{2,26},{3,19},{4,28},{5,21},{6,30},{7,23},{8,16},{9,... | collective-permute-start | bytes 1572872 | tf_op jit(solution)/shard_map/ppermute | solution.py:307
  168.0 55.5 %collective-permute-start.18 = (bf16[4,128,512]{2,1,0:T(8,128)(2,1)}, bf16[4,128,512]{2,1,0:T(8,128)(2,1)}, u32[]{:S(2)}, u32[]{:S(2)}) collective-permute-start(bf16[4,128,512]{2,1,0:T(8,128)(2,1)} %get-tuple-element.204), channel_id=1, source_target_pairs={{0,26},{1,19},{2,24},{3,17},{4,30},{5,23},{6,28},{7,21},{8,18},{9,... | collective-permute-start | bytes 1572872 | tf_op jit(solution)/shard_map/ppermute | solution.py:307
  168.8 62.4 %collective-permute-start.19 = (bf16[4,128,512]{2,1,0:T(8,128)(2,1)}, bf16[4,128,512]{2,1,0:T(8,128)(2,1)}, u32[]{:S(2)}, u32[]{:S(2)}) collective-permute-start(bf16[4,128,512]{2,1,0:T(8,128)(2,1)} %get-tuple-element.203), channel_id=1, source_target_pairs={{0,28},{1,21},{2,30},{3,23},{4,24},{5,17},{6,26},{7,19},{8,20},{9,... | collective-permute-start | bytes 1572872 | tf_op jit(solution)/shard_map/ppermute | solution.py:307
  169.1 67.5 %collective-permute-start.20 = (bf16[4,128,512]{2,1,0:T(8,128)(2,1)}, bf16[4,128,512]{2,1,0:T(8,128)(2,1)}, u32[]{:S(2)}, u32[]{:S(2)}) collective-permute-start(bf16[4,128,512]{2,1,0:T(8,128)(2,1)} %get-tuple-element.202), channel_id=1, source_target_pairs={{0,30},{1,23},{2,28},{3,21},{4,26},{5,19},{6,24},{7,17},{8,22},{9,... | collective-permute-start | bytes 1572872 | tf_op jit(solution)/shard_map/ppermute | solution.py:307
  180.9 3.1 copy-start.8
  180.9 42.6 %copy-start.18 = (bf16[16,2,64,128]{3,2,1,0:T(8,128)(2,1)S(1)}, bf16[16,2,64,128]{3,2,1,0:T(8,128)(2,1)}, u32[]{:S(2)}) copy-start(bf16[16,2,64,128]{3,2,1,0:T(8,128)(2,1)} %constant_dynamic-slice_fusion.18) | copy-start | bytes 1572868
  184.0 127.7 %collective-permute-start.7 = (bf16[3,8,2,2,64,128]{5,4,3,2,1,0:T(8,128)(2,1)S(1)}, bf16[3,8,2,2,64,128]{5,4,3,2,1,0:T(8,128)(2,1)}, u32[]{:S(2)}, u32[]{:S(2)}) collective-permute-start(bf16[3,8,2,2,64,128]{5,4,3,2,1,0:T(8,128)(2,1)S(1)} %copy-done.8), channel_id=1, source_target_pairs={{0,1},{1,0},{2,3},{3,2},{4,5},{5,4},{6,7},{7,6},{8,9},{9,8},{10,11... | collective-permute-start | bytes 4718600 | tf_op jit(solution)/shard_map/ppermute | solution.py:168
  223.6 43.6 %collective-permute-start.23 = (bf16[16,2,64,128]{3,2,1,0:T(8,128)(2,1)S(1)}, bf16[16,2,64,128]{3,2,1,0:T(8,128)(2,1)S(1)}, u32[]{:S(2)}, u32[]{:S(2)}) collective-permute-start(bf16[16,2,64,128]{3,2,1,0:T(8,128)(2,1)S(1)} %copy-done.18), channel_id=1, source_target_pairs={{0,1},{1,0},{2,3},{3,2},{4,5},{5,4},{6,7},{7,6},{8,9},{9,8},{10,11... | collective-permute-start | bytes 1572872 | tf_op jit(solution)/shard_map/ppermute | solution.py:168
  231.3 48.2 %collective-permute-start.3 = (bf16[4,128,512]{2,1,0:T(8,128)(2,1)}, bf16[4,128,512]{2,1,0:T(8,128)(2,1)}, u32[]{:S(2)}, u32[]{:S(2)}) collective-permute-start(bf16[4,128,512]{2,1,0:T(8,128)(2,1)} %get-tuple-element.211), channel_id=1, source_target_pairs={{0,0},{1,9},{2,2},{3,11},{4,4},{5,13},{6,6},{7,15},{8,8},{9,1},{10... | collective-permute-start | bytes 1572872 | tf_op jit(solution)/shard_map/ppermute | solution.py:307
  236.6 43.9 %collective-permute-start.4 = (bf16[4,128,512]{2,1,0:T(8,128)(2,1)}, bf16[4,128,512]{2,1,0:T(8,128)(2,1)}, u32[]{:S(2)}, u32[]{:S(2)}) collective-permute-start(bf16[4,128,512]{2,1,0:T(8,128)(2,1)} %get-tuple-element.210), channel_id=1, source_target_pairs={{0,2},{1,11},{2,0},{3,9},{4,6},{5,15},{6,4},{7,13},{8,10},{9,3},{1... | collective-permute-start | bytes 1572872 | tf_op jit(solution)/shard_map/ppermute | solution.py:307
  246.2 25.0 %copy-start.2 = (bf16[16,128,512]{2,1,0:T(8,128)(2,1)}, bf16[16,128,512]{2,1,0:T(8,128)(2,1)S(1)}, u32[]{:S(2)}) copy-start(bf16[16,128,512]{2,1,0:T(8,128)(2,1)S(1)} %constant_dynamic-update-slice_fusion.10.mixed) | copy-start | bytes 6291460
  267.1 4.1 %copy-start.17 = (bf16[16,2,64,128]{3,2,1,0:T(8,128)(2,1)}, bf16[16,2,64,128]{3,2,1,0:T(8,128)(2,1)S(1)}, u32[]{:S(2)}) copy-start(bf16[16,2,64,128]{3,2,1,0:T(8,128)(2,1)S(1)} %collective-permute-done.23.near_peer) | copy-start | bytes 1572868
  267.1 44.5 %collective-permute-start.9 = (bf16[16,2,64,128]{3,2,1,0:T(8,128)(2,1)}, bf16[16,2,64,128]{3,2,1,0:T(8,128)(2,1)}, u32[]{:S(2)}, u32[]{:S(2)}) collective-permute-start(bf16[16,2,64,128]{3,2,1,0:T(8,128)(2,1)} %constant_dynamic-slice_fusion.15), channel_id=1, source_target_pairs={{0,1},{1,0},{2,3},{3,2},{4,5},{5,4},{6,7},{7,6},{8,9},{9,8},{10,11... | collective-permute-start | bytes 1572872 | tf_op jit(solution)/shard_map/ppermute | solution.py:168
  269.0 2.1 copy-start.6
  269.0 15.2 %collective-permute-start.5 = (bf16[4,128,512]{2,1,0:T(8,128)(2,1)}, bf16[4,128,512]{2,1,0:T(8,128)(2,1)}, u32[]{:S(2)}, u32[]{:S(2)}) collective-permute-start(bf16[4,128,512]{2,1,0:T(8,128)(2,1)} %get-tuple-element.209), channel_id=1, source_target_pairs={{0,4},{1,13},{2,6},{3,15},{4,0},{5,9},{6,2},{7,11},{8,12},{9,5},{1... | collective-permute-start | bytes 1572872 | tf_op jit(solution)/shard_map/ppermute | solution.py:307
  271.2 9.8 %copy-start.9 = (f32[256,256]{1,0:T(8,128)S(1)}, f32[256,256]{1,0:T(8,128)}, u32[]{:S(2)}) copy-start(f32[256,256]{1,0:T(8,128)} %get-tuple-element.215) | copy-start | bytes 786436
  271.2 9.8 %copy-start.10 = (f32[256,256]{1,0:T(8,128)S(1)}, f32[256,256]{1,0:T(8,128)}, u32[]{:S(2)}) copy-start(f32[256,256]{1,0:T(8,128)} %get-tuple-element.216) | copy-start | bytes 786436
  271.2 9.8 %copy-start.11 = (f32[256,256]{1,0:T(8,128)S(1)}, f32[256,256]{1,0:T(8,128)}, u32[]{:S(2)}) copy-start(f32[256,256]{1,0:T(8,128)} %get-tuple-element.217) | copy-start | bytes 786436
  279.5 15.0 %collective-permute-start.6 = (bf16[4,128,512]{2,1,0:T(8,128)(2,1)}, bf16[4,128,512]{2,1,0:T(8,128)(2,1)S(1)}, u32[]{:S(2)}, u32[]{:S(2)}) collective-permute-start(bf16[4,128,512]{2,1,0:T(8,128)(2,1)} %get-tuple-element.208), channel_id=1, source_target_pairs={{0,6},{1,15},{2,4},{3,13},{4,2},{5,11},{6,0},{7,9},{8,14},{9,7},{1... | collective-permute-start | bytes 1572872 | tf_op jit(solution)/shard_map/ppermute | solution.py:307
  280.5 44.9 %collective-permute-start.24 = (bf16[2048,256]{1,0:T(8,128)(2,1)}, bf16[2048,256]{1,0:T(8,128)(2,1)}, u32[]{:S(2)}, u32[]{:S(2)}) collective-permute-start(bf16[2048,256]{1,0:T(8,128)(2,1)} %get-tuple-element.147), channel_id=1, source_target_pairs={{0,1},{1,0},{2,3},{3,2},{4,5},{5,4},{6,7},{7,6},{8,9},{9,8},{10,11... | collective-permute-start | bytes 3145736 | tf_op jit(solution)/shard_map/ppermute | solution.py:168
  281.3 2.9 copy-start.20
  284.3 27.4 %collective-permute-start.8 = (bf16[16,64,128]{2,1,0:T(8,128)(2,1)S(1)}, bf16[16,64,128]{2,1,0:T(8,128)(2,1)S(1)}, u32[]{:S(2)}, u32[]{:S(2)}) collective-permute-start(bf16[16,64,128]{2,1,0:T(8,128)(2,1)S(1)} %copy-done.20), channel_id=1, source_target_pairs={{0,1},{1,0},{2,3},{3,2},{4,5},{5,4},{6,7},{7,6},{8,9},{9,8},{10,11... | collective-permute-start | bytes 786440 | tf_op jit(solution)/shard_map/ppermute | solution.py:168
  294.5 17.2 %copy-start.3 = (bf16[16,128,512]{2,1,0:T(8,128)(2,1)}, bf16[16,128,512]{2,1,0:T(8,128)(2,1)S(1)}, u32[]{:S(2)}) copy-start(bf16[16,128,512]{2,1,0:T(8,128)(2,1)S(1)} %constant_dynamic-update-slice_fusion.18.mixed) | copy-start | bytes 6291460
  311.6 0.7 copy-start.19
  322.6 13.5 %collective-permute-start.27 = (bf16[896,256]{1,0:T(8,128)(2,1)S(1)}, bf16[896,256]{1,0:T(8,128)(2,1)S(1)}, u32[]{:S(2)}, u32[]{:S(2)}) collective-permute-start(bf16[896,256]{1,0:T(8,128)(2,1)S(1)} %get-tuple-element.213), channel_id=1, source_target_pairs={{0,1},{1,0},{2,3},{3,2},{4,5},{5,4},{6,7},{7,6},{8,9},{9,8},{10,11... | collective-permute-start | bytes 1376264 | tf_op jit(solution)/shard_map/ppermute | solution.py:168
  323.3 22.5 %collective-permute-start.28 = (bf16[896,256]{1,0:T(8,128)(2,1)S(1)}, bf16[896,256]{1,0:T(8,128)(2,1)S(1)}, u32[]{:S(2)}, u32[]{:S(2)}) collective-permute-start(bf16[896,256]{1,0:T(8,128)(2,1)S(1)} %get-tuple-element.212), channel_id=1, source_target_pairs={{0,1},{1,0},{2,3},{3,2},{4,5},{5,4},{6,7},{7,6},{8,9},{9,8},{10,11... | collective-permute-start | bytes 1376264 | tf_op jit(solution)/shard_map/ppermute | solution.py:168
  324.7 22.5 %collective-permute-start.29 = (bf16[256,256]{1,0:T(8,128)(2,1)S(1)}, bf16[256,256]{1,0:T(8,128)(2,1)S(1)}, u32[]{:S(2)}, u32[]{:S(2)}) collective-permute-start(bf16[256,256]{1,0:T(8,128)(2,1)S(1)} %slice.212), channel_id=1, source_target_pairs={{0,1},{1,0},{2,3},{3,2},{4,5},{5,4},{6,7},{7,6},{8,9},{9,8},{10,11... | collective-permute-start | bytes 393224 | tf_op jit(solution)/shard_map/ppermute | solution.py:168

commit v3 on v2

--- a/solution.py
+++ b/solution.py
@@ -214,13 +214,13 @@
         "near": (near_t, chunk, 0),
     }
     arrays = {name: entry[0] for name, entry in pool.items()}
-    queue = [(name, s) for s in range(steps) for name in ("source", "rhs", "source_blocks")]
+    queue = [(name, s) for s in range(steps) for name in ("rhs", "source", "source_blocks")]
     for s in range(steps):
         queue += [(name, s) for name in ("target_blocks", "target", "near")]
     queue += ["edges", "ends"]
     first_cut = pl.pallas_call(
         functools.partial(cut_kernel, span=span, masks=[masks[0][0], masks[1][0]]),
-        out_shape=pltpu.VMEM((chunk, half, rows), rhs.dtype),
+        out_shape=pltpu.VMEM((chunk * rows, columns), rhs.dtype),
         in_specs=[pl.BlockSpec(memory_space=pl.ANY)],
         out_specs=pl.BlockSpec(memory_space=pltpu.VMEM),
         scratch_shapes=[pltpu.SemaphoreType.DMA],
@@ -351,13 +351,10 @@
         )
         product, send = far(*operands)
         at = others[s] * (chunk * rows)
-        size = chunk * rows
-        spans = [(0, size)]
-        if s == steps - 1:
-            middle = size // 2
-            spans = [(0, middle - rows), (middle + rows, size), (middle - rows, middle + rows)]
-        for a, b in spans:
-            returned.append((s, swap(send[a:b]), at, a, b))
+        most = chunk * rows if s < steps - 1 else chunk * rows * 7 // 8
+        for a, b in ((0, most), (most, chunk * rows)):
+            if a < b:
+                returned.append((swap(send[a:b]), at, a, b))
 
     own_sums = [edge_sums(near_t, False), jnp.stack(row_sums(near_t, end_rows, high_moved))]
 
@@ -400,9 +397,8 @@
         middle = jnp.zeros(((chunk - 2 * REACH) * rows, columns), jnp.float32)
         added.append(jnp.concatenate([first, middle, last], axis=0))
     added = lax.optimization_barrier(added)
-    for s, part, at, a, b in returned:
-        if a < reach_rows or b > chunk * rows - reach_rows:
-            part = (part.astype(jnp.float32) + added[s][a:b]).astype(rhs.dtype)
+    for s, (part, at, a, b) in zip([*range(steps), steps - 1], returned):
+        part = (part.astype(jnp.float32) + added[s][a:b]).astype(rhs.dtype)
         product = lax.dynamic_update_slice_in_dim(product, part, at + a, 0)
     return product
 

time: 349 us -> 367 us (1.052); the launches traced: 348 us -> 361 us
  waiting for transfers between devices: 154 us -> 181 us
  starting transfers between devices: 103 us -> 87.1 us
    ppermute x8, waiting for transfers between devices: 3.33 us -> 32.8 us  [on_device(): piece = lax.ppermute(cut(mixed, slot, quota), both, pairs)]
    ppermute x8, starting transfers between devices: 25.8 us -> 16.8 us  [on_device(): piece = lax.ppermute(cut(mixed, slot, quota), both, pairs)]
    ppermute x17 -> x16, starting transfers between devices: 69.4 us -> 61.3 us  [swap(): return lax.ppermute(array, 'rhs', SWAP)]
    unnamed x51 -> x73, local copies, waits for them, and re-layouts: 1.19 us -> 8.91 us
    dynamic_update_slice x8, local copies, waits for them, and re-layouts: 7.61 us -> 1.37 us  [on_device(): arrived = lax.dynamic_update_slice_in_dim(arrived, piece, slot * quota, 0)]
    ppermute x17 -> x16, waiting for transfers between devices: 151 us -> 147 us  [swap(): return lax.ppermute(array, 'rhs', SWAP)]
    dynamic_slice x13, local copies, waits for them, and re-layouts: 26.6 us -> 22.8 us  [cut(): return lax.dynamic_slice_in_dim(array, at * size, size, axis)]
  transfers between devices with their start and end apart: 30 -> 29, of which waited for: 10 -> 11; matrix products, arithmetic and copies ran while one was open for 14% -> 14% of each run, Pallas kernels for 9% -> 8%
where the time goes in v3:
time: 367 us; the launch traced here: 361 us
  waiting for transfers between devices  181 us (49%)
  starting transfers between devices  87.1 us (24%)
  local copies, waits for them, and re-layouts  46.6 us (13%)
  Pallas kernels  31.1 us (8%)
  other arithmetic  12.6 us (3%)
    ppermute x16, waiting for transfers between devices, swap(): return lax.ppermute(array, 'rhs', SWAP)  147 us
    ppermute x16, starting transfers between devices, swap(): return lax.ppermute(array, 'rhs', SWAP)  61.3 us
    ppermute x8, waiting for transfers between devices, on_device(): piece = lax.ppermute(cut(mixed, slot, quota), both, pairs)  32.8 us
    dynamic_slice x13, local copies, waits for them, and re-layouts, cut(): return lax.dynamic_slice_in_dim(array, at * size, size, axis)  22.8 us
    ppermute x8, starting transfers between devices, on_device(): piece = lax.ppermute(cut(mixed, slot, quota), both, pairs)  16.8 us
    pallas_call x2, Pallas kernels, on_device(): product, send = far(*operands)  16.2 us
    pallas_call x2, Pallas kernels, on_device(): pl.pallas_call(source_kernel, out_shape=jax.ShapeDtypeStruct((chunk, rank...  13.6 us
    unnamed x73, local copies, waits for them, and re-layouts  8.91 us
  transfers between devices with their start and end apart: 29, of which 11 were waited for; matrix products, arithmetic and copies ran while one was open for 14% of the time, Pallas kernels for 8%

profile of v3, /device:TPU:0, one launch (start us, length us, event | category | flops | bytes accessed | tf_op | source)
XLA Modules:
  0.0 361.1 jit_solution(8913188929684552976)
XLA Ops:
  0.0 1.3 first_cut.1
  2.3 2.8 constant_dynamic-slice_fusion.28
  5.1 2.3 constant_dynamic-slice_fusion.27
  7.3 3.0 collective-permute-start
  11.0 2.8 constant_dynamic-slice_fusion.25
  13.8 2.9 constant_dynamic-slice_fusion.20
  16.8 0.7 constant_dynamic-slice_fusion.19
  17.5 0.9 constant_dynamic-slice_fusion.18
  18.4 2.8 constant_dynamic-slice_fusion.17
  21.9 0.9 constant_dynamic-slice_fusion.15
  22.8 0.7 convert_bitcast_fusion.2
  27.3 1.3 constant_dynamic-update-slice_fusion.4
  31.2 0.8 rev.52
  33.0 1.1 constant_dynamic-slice_fusion.2
  34.1 1.3 collective-permute-start.11
  35.4 3.7 %collective-permute-start.10 = (bf16[256,256]{1,0:T(8,128)(2,1)S(1)}, bf16[256,256]{1,0:T(8,128)(2,1)}, u32[]{:S(2)}, u32[]{:S(2)}) collective-permute-start(bf16[256,256]{1,0:T(8,128)(2,1)S(1)} %get-tuple-element.200), channel_id=1, source_target_pairs={{0,2},{2,4},{4,6},{6,8},{8,10},{10,12},{12,14},{14,16},{16,18},{18... | collective-permute-start | bytes 393224 | tf_op jit(solution)/shard_map/ppermute | solution.py:253
  41.9 0.8 copy.12
  42.7 0.7 reshape.283.offsets
  43.5 1.4 collective-permute-start.25
  44.9 24.6 %collective-permute-done.25 = bf16[6,64,128]{2,1,0:T(8,128)(2,1)S(1)} collective-permute-done((bf16[6,64,128]{2,1,0:T(8,128)(2,1)S(1)}, bf16[6,64,128]{2,1,0:T(8,128)(2,1)S(1)}, u32[]{:S(2)}, u32[]{:S(2)}) %collective-permute-start.25) | collective-permute-done | bytes 98336 | tf_op jit(solution)/shard_map/ppermute | solution.py:168
  69.5 1.7 collective-permute-start.12
  72.4 0.7 reverse_select_fusion.1
  73.3 0.7 reverse_select_fusion.2
  74.3 1.7 collective-permute-start.21
  76.1 0.9 broadcast_select_fusion.4
  78.0 1.7 constant_dynamic-slice_fusion.5
  79.7 1.0 broadcast_select_fusion.1
  80.7 14.8 %collective-permute-done.12.rhs_peer = bf16[2048,256]{1,0:T(8,128)(2,1)S(1)} collective-permute-done((bf16[2048,256]{1,0:T(8,128)(2,1)S(1)}, bf16[2048,256]{1,0:T(8,128)(2,1)S(1)}, u32[]{:S(2)}, u32[]{:S(2)}) %collective-permute-start.12) | collective-permute-done | bytes 1048608 | tf_op jit(solution)/shard_map/ppermute | solution.py:168
  95.5 1.7 collective-permute-start.1
  97.7 0.8 copy-done.27
  99.2 1.3 constant_dynamic-update-slice_fusion.15
  100.5 68.0 %collective-permute-done.1.basis_peer = bf16[16,64,128]{2,1,0:T(8,128)(2,1)S(1)} collective-permute-done((bf16[16,64,128]{2,1,0:T(8,128)(2,1)S(1)}, bf16[16,64,128]{2,1,0:T(8,128)(2,1)S(1)}, u32[]{:S(2)}, u32[]{:S(2)}) %collective-permute-start.1) | collective-permute-done | bytes 262176 | tf_op jit(solution)/shard_map/ppermute | solution.py:168
  168.6 1.7 collective-permute-start.22
  170.6 6.8 %shard_map.91 = bf16[16,128,512]{2,1,0:T(8,128)(2,1)} custom-call(s32[2]{0:T(128)} %pad_add_fusion.idx, bf16[8192,256]{1,0:T(8,128)(2,1)} %rhs_own.3, bf16[2048,256]{1,0:T(8,128)(2,1)} %collective-permute-done.rhs_peer, bf16[64,64,128]{2,1,0:T(8,128)(2,1)} %bitcast.211, bf16[16,64,128]{2,1,0:T(8,128)(2,1)} %copy-done.25, ...), custom_call_target="tpu_custom_call" | custom-call | tf_op jit(solution)/shard_map/pallas_call | solution.py:289
  177.4 2.9 constant_dynamic-slice_fusion.21
  180.3 1.9 collective-permute-start.13
  182.2 5.4 %collective-permute-start.3 = (bf16[4,128,512]{2,1,0:T(8,128)(2,1)}, bf16[4,128,512]{2,1,0:T(8,128)(2,1)}, u32[]{:S(2)}, u32[]{:S(2)}) collective-permute-start(bf16[4,128,512]{2,1,0:T(8,128)(2,1)} %get-tuple-element.213), channel_id=1, source_target_pairs={{0,0},{1,9},{2,2},{3,11},{4,4},{5,13},{6,6},{7,15},{8,8},{9,1},{10... | collective-permute-start | bytes 1572872 | tf_op jit(solution)/shard_map/ppermute | solution.py:307
  187.6 6.8 %shard_map.92 = bf16[16,128,512]{2,1,0:T(8,128)(2,1)} custom-call(s32[2]{0:T(128)} %pad_add_fusion.1.idx, bf16[8192,256]{1,0:T(8,128)(2,1)} %rhs_own.3, bf16[2048,256]{1,0:T(8,128)(2,1)} %copy-done.6, bf16[64,64,128]{2,1,0:T(8,128)(2,1)} %bitcast.212, bf16[16,64,128]{2,1,0:T(8,128)(2,1)} %copy-done.23, bf16[3,32,2,2,64,128]{5,4,3,2,1,0:T(8,128)(2,1)} %own.5, ...), custom_call_target="tpu_custom_call" | custom-call | tf_op jit(solution)/shard_map/pallas_call | solution.py:289
  194.4 1.8 constant_dynamic-slice_fusion.6
  196.2 8.6 %collective-permute-start.17 = (bf16[4,128,512]{2,1,0:T(8,128)(2,1)S(1)}, bf16[4,128,512]{2,1,0:T(8,128)(2,1)S(1)}, u32[]{:S(2)}, u32[]{:S(2)}) collective-permute-start(bf16[4,128,512]{2,1,0:T(8,128)(2,1)S(1)} %get-tuple-element.207), channel_id=1, source_target_pairs={{0,24},{1,17},{2,26},{3,19},{4,28},{5,21},{6,30},{7,23},{8,16},{9,... | collective-permute-start | bytes 1572872 | tf_op jit(solution)/shard_map/ppermute | solution.py:307
  204.8 0.9 fusion.24
  205.9 1.5 collective-permute-start.14
  207.7 1.4 collective-permute-done.14
  209.4 2.6 collective-permute-start.19
  212.0 4.5 %collective-permute-done.17 = bf16[4,128,512]{2,1,0:T(8,128)(2,1)S(1)} collective-permute-done((bf16[4,128,512]{2,1,0:T(8,128)(2,1)S(1)}, bf16[4,128,512]{2,1,0:T(8,128)(2,1)S(1)}, u32[]{:S(2)}, u32[]{:S(2)}) %collective-permute-start.17) | collective-permute-done | bytes 524320 | tf_op jit(solution)/shard_map/ppermute | solution.py:307
  216.5 1.6 constant_dynamic-slice_fusion.4
  218.2 9.6 %collective-permute-done.18 = bf16[4,128,512]{2,1,0:T(8,128)(2,1)S(1)} collective-permute-done((bf16[4,128,512]{2,1,0:T(8,128)(2,1)S(1)}, bf16[4,128,512]{2,1,0:T(8,128)(2,1)S(1)}, u32[]{:S(2)}, u32[]{:S(2)}) %collective-permute-start.18) | collective-permute-done | bytes 524320 | tf_op jit(solution)/shard_map/ppermute | solution.py:307
  228.1 10.9 %collective-permute-done.19 = bf16[4,128,512]{2,1,0:T(8,128)(2,1)S(1)} collective-permute-done((bf16[4,128,512]{2,1,0:T(8,128)(2,1)S(1)}, bf16[4,128,512]{2,1,0:T(8,128)(2,1)S(1)}, u32[]{:S(2)}, u32[]{:S(2)}) %collective-permute-start.19) | collective-permute-done | bytes 524320 | tf_op jit(solution)/shard_map/ppermute | solution.py:307
  239.0 7.8 %collective-permute-done.20 = bf16[4,128,512]{2,1,0:T(8,128)(2,1)S(1)} collective-permute-done((bf16[4,128,512]{2,1,0:T(8,128)(2,1)S(1)}, bf16[4,128,512]{2,1,0:T(8,128)(2,1)S(1)}, u32[]{:S(2)}, u32[]{:S(2)}) %collective-permute-start.20) | collective-permute-done | bytes 524320 | tf_op jit(solution)/shard_map/ppermute | solution.py:307
  246.8 44.4 %collective-permute-start.9 = (bf16[16,2,64,128]{3,2,1,0:T(8,128)(2,1)S(1)}, bf16[16,2,64,128]{3,2,1,0:T(8,128)(2,1)S(1)}, u32[]{:S(2)}, u32[]{:S(2)}) collective-permute-start(bf16[16,2,64,128]{3,2,1,0:T(8,128)(2,1)S(1)} %copy-done.15), channel_id=1, source_target_pairs={{0,1},{1,0},{2,3},{3,2},{4,5},{5,4},{6,7},{7,6},{8,9},{9,8},{10,11... | collective-permute-start | bytes 1572872 | tf_op jit(solution)/shard_map/ppermute | solution.py:168
  291.2 1.3 copy-done.2
  292.5 8.1 %shard_map.93 = (bf16[8192,256]{1,0:T(8,128)(2,1)}, bf16[2048,256]{1,0:T(8,128)(2,1)}) custom-call(s32[2]{0:T(128)} %pad_add_fusion.1.idx, s32[128]{0:T(128)} %reshape.283.offsets, bf16[16,128,512]{2,1,0:T(8,128)(2,1)} %copy-done.2, bf16[3,32,2,2,64,128]{5,4,3,2,1,0:T(8,128)(2,1)} %own.7, bf16[3,8,2,2,64,128]{5,4,3,2,1,0:T(8,128)(2,1)} %copy-done.7, ...), custom_call_target="tpu_custom_call" | custom-call | tf_op jit(solution)/shard_map/pallas_call | solution.py:352
  300.7 0.8 copy-done.16
  301.7 1.1 constant_dynamic-update-slice_fusion.20
  302.8 2.1 collective-permute-start.8
  305.1 24.0 %collective-permute-done.8.basis_peer = bf16[16,64,128]{2,1,0:T(8,128)(2,1)S(1)} collective-permute-done((bf16[16,64,128]{2,1,0:T(8,128)(2,1)S(1)}, bf16[16,64,128]{2,1,0:T(8,128)(2,1)S(1)}, u32[]{:S(2)}, u32[]{:S(2)}) %collective-permute-start.8) | collective-permute-done | bytes 262176 | tf_op jit(solution)/shard_map/ppermute | solution.py:168
  329.9 8.1 %shard_map.94 = (bf16[8192,256]{1,0:T(8,128)(2,1)}, bf16[2048,256]{1,0:T(8,128)(2,1)}) custom-call(s32[2]{0:T(128)} %pad_add_fusion.idx, s32[128]{0:T(128)} %reshape.283.offsets, bf16[16,128,512]{2,1,0:T(8,128)(2,1)} %copy-done.3, bf16[3,32,2,2,64,128]{5,4,3,2,1,0:T(8,128)(2,1)} %own.7, ...), custom_call_target="tpu_custom_call", output_to_operand_aliasing={{0}: (12, {})} | custom-call | tf_op jit(solution)/shard_map/pallas_call | solution.py:352
  338.1 1.2 slice.205
  339.3 1.1 collective-permute-start.27
  340.7 0.9 slice.207
  341.6 1.1 collective-permute-start.28
  342.7 1.2 fusion.3
  343.9 15.1 %collective-permute-done.27 = bf16[1792,256]{1,0:T(8,128)(2,1)S(1)} collective-permute-done((bf16[1792,256]{1,0:T(8,128)(2,1)S(1)}, bf16[1792,256]{1,0:T(8,128)(2,1)S(1)}, u32[]{:S(2)}, u32[]{:S(2)}) %collective-permute-start.27) | collective-permute-done | bytes 917536 | tf_op jit(solution)/shard_map/ppermute | solution.py:168
  359.0 1.1 fusion.4
  (170 shorter events, 19.8 us)
Async XLA Ops:
  0.0 1.5 copy-start.4
  7.3 90.4 %collective-permute-start = (bf16[2048,256]{1,0:T(8,128)(2,1)}, bf16[2048,256]{1,0:T(8,128)(2,1)}, u32[]{:S(2)}, u32[]{:S(2)}) collective-permute-start(bf16[2048,256]{1,0:T(8,128)(2,1)} %constant_dynamic-slice_fusion.27), channel_id=1, source_target_pairs={{0,1},{1,0},{2,3},{3,2},{4,5},{5,4},{6,7},{7,6},{8,9},{9,8},{10,11... | collective-permute-start | bytes 3145736 | tf_op jit(solution)/shard_map/ppermute | solution.py:168
  13.8 3.7 %copy-start.1 = (bf16[64,2,128,64]{2,3,1,0:T(8,128)(2,1)S(1)}, bf16[64,2,128,64]{2,3,1,0:T(8,128)(2,1)}, u32[]{:S(2)}) copy-start(bf16[64,2,128,64]{2,3,1,0:T(8,128)(2,1)} %param.12) | copy-start | bytes 6291460
  13.8 156.5 %collective-permute-start.2 = (bf16[3,8,2,2,64,128]{5,4,3,2,1,0:T(8,128)(2,1)}, bf16[3,8,2,2,64,128]{5,4,3,2,1,0:T(8,128)(2,1)}, u32[]{:S(2)}, u32[]{:S(2)}) collective-permute-start(bf16[3,8,2,2,64,128]{5,4,3,2,1,0:T(8,128)(2,1)} %constant_dynamic-slice_fusion.25), channel_id=1, source_target_pairs={{0,1},{1,0},{2,3},{3,2},{4,5},{5,4},{6,7},{7,6},{8,9},{9,8},{10,11... | collective-permute-start | bytes 4718600 | tf_op jit(solution)/shard_map/ppermute | solution.py:168
  13.8 3.0 copy-start.5
  21.1 2.4 copy-start.29
  29.2 10.6 %copy-start.31 = (s32[2,2]{0,1:T(2,128)S(1)}, s32[2,2]{0,1:T(2,128)}, u32[]{:S(2)}) copy-start(s32[2,2]{0,1:T(2,128)} %get-tuple-element.228) | copy-start | bytes 52
  29.2 10.9 %copy-start.30 = (s32[2,2]{0,1:T(2,128)S(1)}, s32[2,2]{0,1:T(2,128)}, u32[]{:S(2)}) copy-start(s32[2,2]{0,1:T(2,128)} %get-tuple-element.232) | copy-start | bytes 52
  31.1 8.8 %copy-start.19 = (f32[2,2,64,128]{3,2,1,0:T(8,128)S(1)}, f32[2,2,64,128]{3,2,1,0:T(8,128)}, u32[]{:S(2)}) copy-start(f32[2,2,64,128]{3,2,1,0:T(8,128)} %get-tuple-element.201) | copy-start | bytes 393220
  31.2 9.1 %copy-start.18 = (f32[2,2,64,128]{3,2,1,0:T(8,128)S(1)}, f32[2,2,64,128]{3,2,1,0:T(8,128)}, u32[]{:S(2)}) copy-start(f32[2,2,64,128]{3,2,1,0:T(8,128)} %get-tuple-element.203) | copy-start | bytes 393220
  31.2 12.3 %copy-start.32 = (bf16[6,64,128]{2,1,0:T(8,128)(2,1)S(1)}, bf16[6,64,128]{2,1,0:T(8,128)(2,1)}, u32[]{:S(2)}) copy-start(bf16[6,64,128]{2,1,0:T(8,128)(2,1)} %constant_dynamic-update-slice_fusion) | copy-start | bytes 294916
  34.1 39.9 %collective-permute-start.11 = (bf16[256,256]{1,0:T(8,128)(2,1)S(1)}, bf16[256,256]{1,0:T(8,128)(2,1)S(1)}, u32[]{:S(2)}, u32[]{:S(2)}) collective-permute-start(bf16[256,256]{1,0:T(8,128)(2,1)S(1)} %get-tuple-element.199), channel_id=1, source_target_pairs={{2,0},{4,2},{6,4},{8,6},{10,8},{12,10},{14,12},{16,14},{18,16},{20... | collective-permute-start | bytes 393224 | tf_op jit(solution)/shard_map/ppermute | solution.py:253
  35.4 38.9 %collective-permute-start.10 = (bf16[256,256]{1,0:T(8,128)(2,1)S(1)}, bf16[256,256]{1,0:T(8,128)(2,1)}, u32[]{:S(2)}, u32[]{:S(2)}) collective-permute-start(bf16[256,256]{1,0:T(8,128)(2,1)S(1)} %get-tuple-element.200), channel_id=1, source_target_pairs={{0,2},{2,4},{4,6},{6,8},{8,10},{10,12},{12,14},{14,16},{16,18},{18... | collective-permute-start | bytes 393224 | tf_op jit(solution)/shard_map/ppermute | solution.py:253
  39.1 4.3 %collective-permute-start.26 = (bf16[3,64,128]{2,1,0:T(8,128)(2,1)S(1)}, bf16[3,64,128]{2,1,0:T(8,128)(2,1)S(1)}, u32[]{:S(2)}, u32[]{:S(2)}) collective-permute-start(bf16[3,64,128]{2,1,0:T(8,128)(2,1)S(1)} %pad_maximum_fusion.5), channel_id=1, source_target_pairs={{6,7},{9,8},{23,22},{24,25}} | collective-permute-start | bytes 147464 | tf_op jit(solution)/shard_map/ppermute | solution.py:240
  43.5 26.0 %collective-permute-start.25 = (bf16[6,64,128]{2,1,0:T(8,128)(2,1)S(1)}, bf16[6,64,128]{2,1,0:T(8,128)(2,1)S(1)}, u32[]{:S(2)}, u32[]{:S(2)}) collective-permute-start(bf16[6,64,128]{2,1,0:T(8,128)(2,1)S(1)} %copy-done.32), channel_id=1, source_target_pairs={{0,1},{1,0},{2,3},{3,2},{4,5},{5,4},{6,7},{7,6},{8,9},{9,8},{10,11... | collective-permute-start | bytes 294920 | tf_op jit(solution)/shard_map/ppermute | solution.py:168
  69.5 26.0 %collective-permute-start.12 = (bf16[2048,256]{1,0:T(8,128)(2,1)S(1)}, bf16[2048,256]{1,0:T(8,128)(2,1)S(1)}, u32[]{:S(2)}, u32[]{:S(2)}) collective-permute-start(bf16[2048,256]{1,0:T(8,128)(2,1)S(1)} %first_cut.1), channel_id=1, source_target_pairs={{0,1},{1,0},{2,3},{3,2},{4,5},{5,4},{6,7},{7,6},{8,9},{9,8},{10,11... | collective-permute-start | bytes 3145736 | tf_op jit(solution)/shard_map/ppermute | solution.py:168
  71.3 5.7 %copy-start = (bf16[8192,256]{1,0:T(8,128)(2,1)S(1)}, bf16[8192,256]{1,0:T(8,128)(2,1)}, u32[]{:S(2)}) copy-start(bf16[8192,256]{1,0:T(8,128)(2,1)} %rhs_own.3) | copy-start | bytes 12582916
  74.0 108.2 %collective-permute-start.16 = (bf16[3,8,2,2,64,128]{5,4,3,2,1,0:T(8,128)(2,1)}, bf16[3,8,2,2,64,128]{5,4,3,2,1,0:T(8,128)(2,1)}, u32[]{:S(2)}, u32[]{:S(2)}) collective-permute-start(bf16[3,8,2,2,64,128]{5,4,3,2,1,0:T(8,128)(2,1)} %constant_dynamic-slice_fusion.28), channel_id=1, source_target_pairs={{0,1},{1,0},{2,3},{3,2},{4,5},{5,4},{6,7},{7,6},{8,9},{9,8},{10,11... | collective-permute-start | bytes 4718600 | tf_op jit(solution)/shard_map/ppermute | solution.py:168
  74.3 134.8 %collective-permute-start.21 = (bf16[3,8,2,2,64,128]{5,4,3,2,1,0:T(8,128)(2,1)}, bf16[3,8,2,2,64,128]{5,4,3,2,1,0:T(8,128)(2,1)S(1)}, u32[]{:S(2)}, u32[]{:S(2)}) collective-permute-start(bf16[3,8,2,2,64,128]{5,4,3,2,1,0:T(8,128)(2,1)} %constant_dynamic-slice_fusion.20), channel_id=1, source_target_pairs={{0,1},{1,0},{2,3},{3,2},{4,5},{5,4},{6,7},{7,6},{8,9},{9,8},{10,11... | collective-permute-start | bytes 4718600 | tf_op jit(solution)/shard_map/ppermute | solution.py:168
  78.0 17.6 %copy-start.28 = (bf16[16,64,128]{2,1,0:T(8,128)(2,1)S(1)}, bf16[16,64,128]{2,1,0:T(8,128)(2,1)}, u32[]{:S(2)}) copy-start(bf16[16,64,128]{2,1,0:T(8,128)(2,1)} %constant_dynamic-slice_fusion.26) | copy-start | bytes 786436
  95.5 2.1 copy-start.6
  95.5 73.0 %collective-permute-start.1 = (bf16[16,64,128]{2,1,0:T(8,128)(2,1)S(1)}, bf16[16,64,128]{2,1,0:T(8,128)(2,1)S(1)}, u32[]{:S(2)}, u32[]{:S(2)}) collective-permute-start(bf16[16,64,128]{2,1,0:T(8,128)(2,1)S(1)} %copy-done.28), channel_id=1, source_target_pairs={{0,1},{1,0},{2,3},{3,2},{4,5},{5,4},{6,7},{7,6},{8,9},{9,8},{10,11... | collective-permute-start | bytes 786440 | tf_op jit(solution)/shard_map/ppermute | solution.py:168
  97.6 1.0 copy-start.27
  98.6 81.7 %collective-permute-start.15 = (bf16[16,64,128]{2,1,0:T(8,128)(2,1)S(1)}, bf16[16,64,128]{2,1,0:T(8,128)(2,1)S(1)}, u32[]{:S(2)}, u32[]{:S(2)}) collective-permute-start(bf16[16,64,128]{2,1,0:T(8,128)(2,1)S(1)} %copy-done.27), channel_id=1, source_target_pairs={{0,1},{1,0},{2,3},{3,2},{4,5},{5,4},{6,7},{7,6},{8,9},{9,8},{10,11... | collective-permute-start | bytes 786440 | tf_op jit(solution)/shard_map/ppermute | solution.py:168
  168.6 2.0 copy-start.25
  168.6 37.2 %collective-permute-start.22 = (bf16[16,64,128]{2,1,0:T(8,128)(2,1)}, bf16[16,64,128]{2,1,0:T(8,128)(2,1)S(1)}, u32[]{:S(2)}, u32[]{:S(2)}) collective-permute-start(bf16[16,64,128]{2,1,0:T(8,128)(2,1)} %constant_dynamic-slice_fusion.19), channel_id=1, source_target_pairs={{0,1},{1,0},{2,3},{3,2},{4,5},{5,4},{6,7},{7,6},{8,9},{9,8},{10,11... | collective-permute-start | bytes 786440 | tf_op jit(solution)/shard_map/ppermute | solution.py:168
  170.3 35.5 %collective-permute-start.23 = (bf16[16,2,64,128]{3,2,1,0:T(8,128)(2,1)}, bf16[16,2,64,128]{3,2,1,0:T(8,128)(2,1)S(1)}, u32[]{:S(2)}, u32[]{:S(2)}) collective-permute-start(bf16[16,2,64,128]{3,2,1,0:T(8,128)(2,1)} %constant_dynamic-slice_fusion.18), channel_id=1, source_target_pairs={{0,1},{1,0},{2,3},{3,2},{4,5},{5,4},{6,7},{7,6},{8,9},{9,8},{10,11... | collective-permute-start | bytes 1572872 | tf_op jit(solution)/shard_map/ppermute | solution.py:168
  180.3 7.3 %copy-start.23 = (bf16[16,64,128]{2,1,0:T(8,128)(2,1)}, bf16[16,64,128]{2,1,0:T(8,128)(2,1)S(1)}, u32[]{:S(2)}) copy-start(bf16[16,64,128]{2,1,0:T(8,128)(2,1)S(1)} %collective-permute-done.15.basis_peer) | copy-start | bytes 786436
  180.3 15.9 %collective-permute-start.13 = (bf16[256,256]{1,0:T(8,128)(2,1)S(1)}, bf16[256,256]{1,0:T(8,128)(2,1)}, u32[]{:S(2)}, u32[]{:S(2)}) collective-permute-start(bf16[256,256]{1,0:T(8,128)(2,1)S(1)} %slice.215), channel_id=1, source_target_pairs={{0,2},{2,4},{4,6},{9,11},{11,13},{13,15},{15,17},{17,19},{19,21},{... | collective-permute-start | bytes 393224 | tf_op jit(solution)/shard_map/ppermute | solution.py:256
  182.2 27.1 %collective-permute-start.3 = (bf16[4,128,512]{2,1,0:T(8,128)(2,1)}, bf16[4,128,512]{2,1,0:T(8,128)(2,1)}, u32[]{:S(2)}, u32[]{:S(2)}) collective-permute-start(bf16[4,128,512]{2,1,0:T(8,128)(2,1)} %get-tuple-element.213), channel_id=1, source_target_pairs={{0,0},{1,9},{2,2},{3,11},{4,4},{5,13},{6,6},{7,15},{8,8},{9,1},{10... | collective-permute-start | bytes 1572872 | tf_op jit(solution)/shard_map/ppermute | solution.py:307
  194.4 13.0 %copy-start.8 = (f32[2,128,256]{2,1,0:T(8,128)S(1)}, f32[2,128,256]{2,1,0:T(8,128)}, u32[]{:S(2)}) copy-start(f32[2,128,256]{2,1,0:T(8,128)} %reverse_select_fusion.1) | copy-start | bytes 786436
  194.4 13.0 %copy-start.9 = (f32[2,128,256]{2,1,0:T(8,128)S(1)}, f32[2,128,256]{2,1,0:T(8,128)}, u32[]{:S(2)}) copy-start(f32[2,128,256]{2,1,0:T(8,128)} %reverse_select_fusion.2) | copy-start | bytes 786436
  194.4 13.0 %copy-start.10 = (f32[2,128,256]{2,1,0:T(8,128)S(1)}, f32[2,128,256]{2,1,0:T(8,128)}, u32[]{:S(2)}) copy-start(f32[2,128,256]{2,1,0:T(8,128)} %get-tuple-element.218) | copy-start | bytes 786436
  194.4 13.0 %copy-start.11 = (f32[2,128,256]{2,1,0:T(8,128)S(1)}, f32[2,128,256]{2,1,0:T(8,128)}, u32[]{:S(2)}) copy-start(f32[2,128,256]{2,1,0:T(8,128)} %get-tuple-element.219) | copy-start | bytes 786436
  194.4 13.0 %copy-start.12 = (f32[2,128,256]{2,1,0:T(8,128)S(1)}, f32[2,128,256]{2,1,0:T(8,128)}, u32[]{:S(2)}) copy-start(f32[2,128,256]{2,1,0:T(8,128)} %get-tuple-element.220) | copy-start | bytes 786436
  194.4 13.0 %copy-start.13 = (f32[2,128,256]{2,1,0:T(8,128)S(1)}, f32[2,128,256]{2,1,0:T(8,128)}, u32[]{:S(2)}) copy-start(f32[2,128,256]{2,1,0:T(8,128)} %get-tuple-element.221) | copy-start | bytes 786436
  196.2 20.3 %collective-permute-start.17 = (bf16[4,128,512]{2,1,0:T(8,128)(2,1)S(1)}, bf16[4,128,512]{2,1,0:T(8,128)(2,1)S(1)}, u32[]{:S(2)}, u32[]{:S(2)}) collective-permute-start(bf16[4,128,512]{2,1,0:T(8,128)(2,1)S(1)} %get-tuple-element.207), channel_id=1, source_target_pairs={{0,24},{1,17},{2,26},{3,19},{4,28},{5,21},{6,30},{7,23},{8,16},{9,... | collective-permute-start | bytes 1572872 | tf_op jit(solution)/shard_map/ppermute | solution.py:307
  205.8 1.6 copy-start.22
  205.8 123.3 %collective-permute-start.7 = (bf16[3,8,2,2,64,128]{5,4,3,2,1,0:T(8,128)(2,1)}, bf16[3,8,2,2,64,128]{5,4,3,2,1,0:T(8,128)(2,1)}, u32[]{:S(2)}, u32[]{:S(2)}) collective-permute-start(bf16[3,8,2,2,64,128]{5,4,3,2,1,0:T(8,128)(2,1)} %constant_dynamic-slice_fusion.17), channel_id=1, source_target_pairs={{0,1},{1,0},{2,3},{3,2},{4,5},{5,4},{6,7},{7,6},{8,9},{9,8},{10,11... | collective-permute-start | bytes 4718600 | tf_op jit(solution)/shard_map/ppermute | solution.py:168
  205.9 1.5 copy-start.14
  205.9 3.2 collective-permute-start.14
  209.1 18.6 %collective-permute-start.18 = (bf16[4,128,512]{2,1,0:T(8,128)(2,1)S(1)}, bf16[4,128,512]{2,1,0:T(8,128)(2,1)S(1)}, u32[]{:S(2)}, u32[]{:S(2)}) collective-permute-start(bf16[4,128,512]{2,1,0:T(8,128)(2,1)S(1)} %get-tuple-element.206), channel_id=1, source_target_pairs={{0,26},{1,19},{2,24},{3,17},{4,30},{5,23},{6,28},{7,21},{8,18},{9,... | collective-permute-start | bytes 1572872 | tf_op jit(solution)/shard_map/ppermute | solution.py:307
  209.2 9.0 %copy-start.7 = (bf16[3,8,2,2,64,128]{5,4,3,2,1,0:T(8,128)(2,1)}, bf16[3,8,2,2,64,128]{5,4,3,2,1,0:T(8,128)(2,1)S(1)}, u32[]{:S(2)}) copy-start(bf16[3,8,2,2,64,128]{5,4,3,2,1,0:T(8,128)(2,1)S(1)} %collective-permute-done.21.peer) | copy-start | bytes 4718596
  209.2 91.5 %collective-permute-start.4 = (bf16[4,128,512]{2,1,0:T(8,128)(2,1)}, bf16[4,128,512]{2,1,0:T(8,128)(2,1)S(1)}, u32[]{:S(2)}, u32[]{:S(2)}) collective-permute-start(bf16[4,128,512]{2,1,0:T(8,128)(2,1)} %get-tuple-element.212), channel_id=1, source_target_pairs={{0,2},{1,11},{2,0},{3,9},{4,6},{5,15},{6,4},{7,13},{8,10},{9,3},{1... | collective-permute-start | bytes 1572872 | tf_op jit(solution)/shard_map/ppermute | solution.py:307
  209.4 29.6 %collective-permute-start.19 = (bf16[4,128,512]{2,1,0:T(8,128)(2,1)S(1)}, bf16[4,128,512]{2,1,0:T(8,128)(2,1)S(1)}, u32[]{:S(2)}, u32[]{:S(2)}) collective-permute-start(bf16[4,128,512]{2,1,0:T(8,128)(2,1)S(1)} %get-tuple-element.205), channel_id=1, source_target_pairs={{0,28},{1,21},{2,30},{3,23},{4,24},{5,17},{6,26},{7,19},{8,20},{9,... | collective-permute-start | bytes 1572872 | tf_op jit(solution)/shard_map/ppermute | solution.py:307
  216.5 30.3 %collective-permute-start.20 = (bf16[4,128,512]{2,1,0:T(8,128)(2,1)S(1)}, bf16[4,128,512]{2,1,0:T(8,128)(2,1)S(1)}, u32[]{:S(2)}, u32[]{:S(2)}) collective-permute-start(bf16[4,128,512]{2,1,0:T(8,128)(2,1)S(1)} %get-tuple-element.204), channel_id=1, source_target_pairs={{0,30},{1,23},{2,28},{3,21},{4,26},{5,19},{6,24},{7,17},{8,22},{9,... | collective-permute-start | bytes 1572872 | tf_op jit(solution)/shard_map/ppermute | solution.py:307
  227.8 11.2 %copy-start.20 = (bf16[4,128,512]{2,1,0:T(8,128)(2,1)S(1)}, bf16[4,128,512]{2,1,0:T(8,128)(2,1)}, u32[]{:S(2)}) copy-start(bf16[4,128,512]{2,1,0:T(8,128)(2,1)} %get-tuple-element.210) | copy-start | bytes 1572868
  227.8 75.0 %collective-permute-start.5 = (bf16[4,128,512]{2,1,0:T(8,128)(2,1)}, bf16[4,128,512]{2,1,0:T(8,128)(2,1)S(1)}, u32[]{:S(2)}, u32[]{:S(2)}) collective-permute-start(bf16[4,128,512]{2,1,0:T(8,128)(2,1)} %get-tuple-element.211), channel_id=1, source_target_pairs={{0,4},{1,13},{2,6},{3,15},{4,0},{5,9},{6,2},{7,11},{8,12},{9,5},{1... | collective-permute-start | bytes 1572872 | tf_op jit(solution)/shard_map/ppermute | solution.py:307
  228.0 18.8 %copy-start.15 = (bf16[16,2,64,128]{3,2,1,0:T(8,128)(2,1)S(1)}, bf16[16,2,64,128]{3,2,1,0:T(8,128)(2,1)}, u32[]{:S(2)}) copy-start(bf16[16,2,64,128]{3,2,1,0:T(8,128)(2,1)} %constant_dynamic-slice_fusion.15) | copy-start | bytes 1572868
  239.0 66.0 %collective-permute-start.6 = (bf16[4,128,512]{2,1,0:T(8,128)(2,1)S(1)}, bf16[4,128,512]{2,1,0:T(8,128)(2,1)S(1)}, u32[]{:S(2)}, u32[]{:S(2)}) collective-permute-start(bf16[4,128,512]{2,1,0:T(8,128)(2,1)S(1)} %copy-done.20), channel_id=1, source_target_pairs={{0,6},{1,15},{2,4},{3,13},{4,2},{5,11},{6,0},{7,9},{8,14},{9,7},{1... | collective-permute-start | bytes 1572872 | tf_op jit(solution)/shard_map/ppermute | solution.py:307
  246.8 82.2 %collective-permute-start.9 = (bf16[16,2,64,128]{3,2,1,0:T(8,128)(2,1)S(1)}, bf16[16,2,64,128]{3,2,1,0:T(8,128)(2,1)S(1)}, u32[]{:S(2)}, u32[]{:S(2)}) collective-permute-start(bf16[16,2,64,128]{3,2,1,0:T(8,128)(2,1)S(1)} %copy-done.15), channel_id=1, source_target_pairs={{0,1},{1,0},{2,3},{3,2},{4,5},{5,4},{6,7},{7,6},{8,9},{9,8},{10,11... | collective-permute-start | bytes 1572872 | tf_op jit(solution)/shard_map/ppermute | solution.py:168
  291.2 1.3 copy-start.2
  300.7 2.1 copy-start.26
  300.7 0.8 copy-start.16
  301.5 3.4 copy-start.17
  301.5 41.2 %collective-permute-start.24 = (bf16[2048,256]{1,0:T(8,128)(2,1)}, bf16[2048,256]{1,0:T(8,128)(2,1)S(1)}, u32[]{:S(2)}, u32[]{:S(2)}) collective-permute-start(bf16[2048,256]{1,0:T(8,128)(2,1)} %get-tuple-element.149), channel_id=1, source_target_pairs={{0,1},{1,0},{2,3},{3,2},{4,5},{5,4},{6,7},{7,6},{8,9},{9,8},{10,11... | collective-permute-start | bytes 3145736 | tf_op jit(solution)/shard_map/ppermute | solution.py:168
  302.8 26.2 %collective-permute-start.8 = (bf16[16,64,128]{2,1,0:T(8,128)(2,1)S(1)}, bf16[16,64,128]{2,1,0:T(8,128)(2,1)S(1)}, u32[]{:S(2)}, u32[]{:S(2)}) collective-permute-start(bf16[16,64,128]{2,1,0:T(8,128)(2,1)S(1)} %copy-done.26), channel_id=1, source_target_pairs={{0,1},{1,0},{2,3},{3,2},{4,5},{5,4},{6,7},{7,6},{8,9},{9,8},{10,11... | collective-permute-start | bytes 786440 | tf_op jit(solution)/shard_map/ppermute | solution.py:168
  305.1 24.0 %copy-start.3 = (bf16[16,128,512]{2,1,0:T(8,128)(2,1)}, bf16[16,128,512]{2,1,0:T(8,128)(2,1)S(1)}, u32[]{:S(2)}) copy-start(bf16[16,128,512]{2,1,0:T(8,128)(2,1)S(1)} %constant_dynamic-update-slice_fusion.17.mixed) | copy-start | bytes 6291460
  329.0 0.7 copy-start.24
  329.0 0.9 copy-start.21
  339.3 19.7 %collective-permute-start.27 = (bf16[1792,256]{1,0:T(8,128)(2,1)S(1)}, bf16[1792,256]{1,0:T(8,128)(2,1)S(1)}, u32[]{:S(2)}, u32[]{:S(2)}) collective-permute-start(bf16[1792,256]{1,0:T(8,128)(2,1)S(1)} %slice.205), channel_id=1, source_target_pairs={{0,1},{1,0},{2,3},{3,2},{4,5},{5,4},{6,7},{7,6},{8,9},{9,8},{10,11... | collective-permute-start | bytes 2752520 | tf_op jit(solution)/shard_map/ppermute | solution.py:168
  341.6 18.8 %collective-permute-start.28 = (bf16[256,256]{1,0:T(8,128)(2,1)S(1)}, bf16[256,256]{1,0:T(8,128)(2,1)S(1)}, u32[]{:S(2)}, u32[]{:S(2)}) collective-permute-start(bf16[256,256]{1,0:T(8,128)(2,1)S(1)} %slice.207), channel_id=1, source_target_pairs={{0,1},{1,0},{2,3},{3,2},{4,5},{5,4},{6,7},{7,6},{8,9},{9,8},{10,11... | collective-permute-start | bytes 393224 | tf_op jit(solution)/shard_map/ppermute | solution.py:168
